TPU v7x, 32 devices: a whole 2x2x4 slice. The times are simulated.
32 devices in a mesh: grp: 16 (over z, x, core), slab: 2 (over y).
Axes of the slice: x: 2, y: 2, z: 4, core: 2. Of those that a mesh axis runs over, the one named last changes fastest.
Arguments:
- ligand_grids: float32 [2, 4, 128, 128, 128], P(None, None, 'grp', 'slab'), may hold values from -6 to 6
- receptor_kernel: bfloat16 [16, 2, 2, 128, 128, 128], P('grp', None, None, 'slab'), may hold values from -3 to 3
Outputs:
- best_score: bfloat16 [16, 128, 128, 128], P('grp', None, 'slab')
All inputs are finite; a program needn't handle non-finite values.
Results may differ from a plain program's by a relative error of at most 0.018.
Values may be sent and summed in bfloat16 or wider, within the bound.
A program may use at most 128 MiB of HBM per device.

v0:
```python
import math

import functools

import jax
import jax.numpy as jnp
import numpy as np
from jax import lax
from jax.experimental import pallas as pl
from jax.experimental.pallas import tpu as pltpu
from jax.sharding import PartitionSpec as P

highest = lax.Precision.HIGHEST


def coefficients(length, inverse):
    positions = jnp.arange(length, dtype=jnp.int32)
    phases = positions[:, None] * positions[None, :] % length
    angles = phases.astype(jnp.float32) * (2.0 * math.pi / length)
    scaling = 1.0 / math.sqrt(length)
    cosine = jnp.cos(angles) * scaling
    sine_part = jnp.sin(angles) * scaling
    if inverse:
        sine_part = -sine_part
    upper_rows = jnp.stack([cosine, sine_part])
    lower_rows = jnp.stack([-sine_part, cosine])
    return jnp.stack([upper_rows, lower_rows])


def pack_pairs(ligand_piece):
    stacked = jnp.stack([ligand_piece[:, 0::2], ligand_piece[:, 1::2]])
    return stacked.reshape((2, stacked.shape[1] * stacked.shape[2]) + stacked.shape[3:])


def body(ligand_grids, receptor_kernel):
    length = ligand_grids.shape[4]
    rotations = ligand_grids.shape[0]
    channel_pairs = ligand_grids.shape[1] // 2
    forward = coefficients(length, False)
    forward_low = forward.astype(jnp.bfloat16)
    inverse_low = coefficients(length, True).astype(jnp.bfloat16)
    packed = pack_pairs(ligand_grids)
    lines = jnp.einsum("pqkn,qrzxn->pkrzx", forward, packed, precision=highest)
    columns = lax.all_to_all(
        lines.astype(jnp.bfloat16), "grp", split_axis=1, concat_axis=3, tiled=True
    ).astype(lines.dtype)
    partial_value = jnp.einsum("pqkn,qyrnx->pyrkx", forward, columns, precision=highest).astype(
        jnp.bfloat16
    )
    pieces = jnp.einsum(
        "pqkn,qyrzn->pyrzk",
        forward_low,
        lax.all_to_all(partial_value, "slab", split_axis=3, concat_axis=4, tiled=True),
        preferred_element_type=jnp.float32,
    ).astype(jnp.bfloat16)
    collected = lax.all_gather(pieces, "grp", axis=1, tiled=True)
    spectrum = jnp.transpose(collected, (0, 2, 3, 4, 1))
    spec_split = spectrum.reshape((2, rotations, channel_pairs) + spectrum.shape[2:])
    kernel_one = receptor_kernel[0]
    kernel_real = kernel_one[0][None].astype(jnp.float32)
    kernel_imag = kernel_one[1][None].astype(jnp.float32)
    spec_real = spec_split[0].astype(jnp.float32)
    spec_imag = spec_split[1].astype(jnp.float32)
    real_part = jnp.sum(kernel_real * spec_real - kernel_imag * spec_imag, axis=1)
    imag_part = jnp.sum(kernel_real * spec_imag + kernel_imag * spec_real, axis=1)
    product = jnp.stack([real_part, imag_part]).astype(jnp.bfloat16)
    rows_done = jnp.einsum(
        "pqkn,qrznm->przkm", inverse_low, product, preferred_element_type=jnp.float32
    ).astype(jnp.bfloat16)
    planes = jnp.einsum(
        "pqkn,qrzxn->przxk", inverse_low, rows_done, preferred_element_type=jnp.float32
    ).astype(jnp.bfloat16)
    scores = jnp.einsum(
        "qkn,qrnxy->rkxy",
        inverse_low[0],
        lax.all_to_all(planes, "slab", split_axis=3, concat_axis=2, tiled=True),
        preferred_element_type=jnp.float32,
    )
    return jnp.max(scores, axis=0).astype(jnp.bfloat16)[None]


TILE = 16
SUB = 8
f32 = jnp.float32
bf16 = jnp.bfloat16


def waves(length):
    positions = np.arange(length)
    angles = (positions[:, None] * positions[None, :] % length) * (2.0 * math.pi / length)
    scaling = 1.0 / math.sqrt(length)
    cosine, sine = np.cos(angles) * scaling, np.sin(angles) * scaling
    forward = np.stack([np.stack([cosine, sine]), np.stack([-sine, cosine])])
    inverse = np.stack([np.stack([cosine, -sine]), np.stack([sine, cosine])])
    return forward, inverse


def matrices(length, groups):
    forward, inverse = waves(length)
    half, side = length // 2, 2 * length
    block = half // groups
    fz, fx, ix, mz = [], [], [], []
    for own in range(2):
        order = (np.arange(length) + own * half) % length
        by_cell = forward[:, :, order].reshape(2, 2, length, groups, length // groups)
        fz.append(by_cell.transpose(0, 2, 3, 1, 4).reshape(side, side))
        cells = forward[:, :, :, order].reshape(2, 2, length, 2, groups, block)
        fx.append(cells.transpose(0, 2, 4, 3, 1, 5).reshape(side, side))
        ix.append(inverse[:, :, order].transpose(0, 2, 1, 3).reshape(side, side))
        lines = inverse[0][:, :, order].reshape(2, length, length // SUB, SUB)
        mz.append(lines.transpose(1, 2, 0, 3).reshape(length, side))
    fy = forward.transpose(1, 3, 0, 2).reshape(side, side)
    iy = inverse.transpose(1, 3, 0, 2).reshape(side, side)
    return [np.stack(m).astype(np.float32) for m in (fz, fx, ix, mz)] + [
        fy.astype(np.float32),
        iy.astype(np.float32),
    ]


def dot(a, b):
    return jnp.dot(a, b, preferred_element_type=f32)


def split_kernel(rotations, pairs, depth, width, block, lig_ref, out_ref):
    @pl.loop(0, width)
    def _(x):
        for r in range(rotations):
            for j in range(pairs):
                parts = []
                for q in range(2):
                    first = ((r * pairs + j) * 2 + q) * depth * width
                    parts.append(lig_ref[pl.ds(first + x, depth, stride=width), :])
                out_ref[x // block, x % block, r * pairs + j] = jnp.concatenate(parts, 0).astype(bf16)


def zy_kernel(rotations, groups, block, length, fz_ref, fy_ref, in_ref, mine_ref, other_ref, hold):
    fz = fz_ref[...]
    fy = fy_ref[...]
    grids = 2 * rotations

    @pl.loop(0, block)
    def _(x):
        for r in range(rotations):
            cols = [
                jnp.concatenate([in_ref[g, x, 2 * r + j] for g in range(groups)], 0) for j in range(2)
            ]
            lines = dot(fz, jnp.concatenate(cols, 1)).astype(bf16)
            rows = []
            for j in range(2):
                at = slice(j * length, (j + 1) * length)
                rows.append(jnp.concatenate([lines[:length, at], lines[length:, at]], 1))
            plane = dot(jnp.concatenate(rows, 0), fy)
            for p in range(2):
                start = ((p * block + x) * grids + 2 * r) * length
                hold[pl.ds(start, 2 * length), :] = plane[:, p * length : (p + 1) * length]

    stride = grids * length
    half = length // 2

    @pl.loop(0, half, unroll=2)
    def _(k):
        for i in range(grids):
            mine_ref[k, i] = hold[pl.ds(i * length + k, 2 * block, stride=stride), :].astype(bf16)
            other_ref[k, i] = hold[pl.ds(i * length + half + k, 2 * block, stride=stride), :].astype(
                bf16
            )


def score_kernel(
    rotations, groups, length, chunks, fx_ref, ix_ref, iy_ref, mz_ref, rec_ref, near_ref, swap_ref, out_ref,
    mine_ref, far_ref, held, came, rec, send, hold, rec_sem, swap_out, swap_in, ring_out, ring_in, pair_out, pair_in, slab_out, slab_in,
):
    me = lax.axis_index("grp")
    slab = lax.axis_index("slab")
    core = lax.rem(me, 2)
    height = groups // 4
    around = groups // 2
    row = me // 4
    column = lax.rem(me // 2, 2)
    spot = jnp.where(column == 0, row, around - 1 - row)

    def device(at, which):
        at = lax.rem(at + around, around)
        return jnp.where(at < height, at * 4, (around - 1 - at) * 4 + 2) + which

    beside = (device(spot + 1, core), device(spot - 1, core))
    partner = device(spot, 1 - core)

    def place(to):
        return {"grp": to, "slab": slab}

    across = {"grp": me, "slab": 1 - slab}
    MESH = pl.DeviceIdType.MESH
    load = pltpu.make_async_copy(rec_ref, rec, rec_sem)
    load.start()
    barrier = pltpu.get_barrier_semaphore()
    for to in (place(beside[0]), place(beside[1]), place(partner), across):
        pl.semaphore_signal(barrier, inc=1, device_id=to, device_id_type=MESH)
    pl.semaphore_wait(barrier, 4)

    def swap(c):
        at = pl.ds(c * SUB, SUB)
        return pltpu.make_async_remote_copy(
            src_ref=swap_ref.at[at], dst_ref=came.at[at],
            send_sem=swap_out.at[c], recv_sem=swap_in.at[c],
            device_id=across, device_id_type=MESH,
        )

    @pl.loop(0, chunks)
    def _(c):
        swap(c).start()

    def join(c):
        swap(c).wait_recv()

        @pl.loop(0, SUB)
        def _(k):
            z = c * SUB + k
            for g in range(near_ref.shape[1]):
                both = [near_ref[z, g].astype(f32), came[z, g].astype(f32)]
                held[me, z, g] = jnp.concatenate(both, 0).astype(bf16)

    def origin(d, t):
        return spot - t if d == 0 else spot + t

    def part(slot, c):
        return held.at[slot, pl.ds(c * SUB, SUB)]

    def ring(d, c, t, slot):
        return pltpu.make_async_remote_copy(
            src_ref=part(slot, c), dst_ref=part(slot, c),
            send_sem=ring_out.at[d, c, t], recv_sem=ring_in.at[d, c, t],
            device_id=place(beside[d]), device_id_type=MESH,
        )

    def ring_send(d, c, t):
        ring(d, c, t, device(origin(d, t), core)).start()

    def ring_wait(d, c, t):
        ring(d, c, t, device(origin(d, t + 1), core)).wait_recv()

    def pair(d, c, t, which):
        slot = device(origin(d, t), which)
        return pltpu.make_async_remote_copy(
            src_ref=part(slot, c), dst_ref=part(slot, c),
            send_sem=pair_out.at[d, c, t], recv_sem=pair_in.at[d, c, t],
            device_id=place(partner), device_id_type=MESH,
        )

    def slab_copy(c, q):
        at = pl.ds(pl.multiple_of(q * TILE, TILE), TILE)
        return pltpu.make_async_remote_copy(
            src_ref=send.at[c, :, at], dst_ref=far_ref.at[c, :, at],
            send_sem=slab_out.at[c, q], recv_sem=slab_in.at[c, q],
            device_id=across, device_id_type=MESH,
        )

    far_step = around // 2 - 1

    def for_far(c, act):
        for d in range(2):
            @pl.when(lax.rem(c, 2) == d)
            def _():
                act(d)

    def arrived(c, t):
        for d in range(2):
            ring_wait(d, c, t)
            if t + 1 < far_step:
                ring_send(d, c, t + 1)
            pair(d, c, t + 1, core).start()

    rows = rotations * length
    half = length // 2

    def compute(c, first):
        @pl.loop(first, first + SUB // 2, unroll=2)
        def _(k):
            z = c * SUB + k
            kr = [rec[0, j, z].astype(f32) for j in range(2)]
            ki = [rec[1, j, z].astype(f32) for j in range(2)]
            real, imag = [], []
            for r in range(rotations):
                cols = [
                    jnp.concatenate([held[g, z, 2 * r + j] for g in range(groups)], 0)
                    for j in range(2)
                ]
                spec = dot(fx_ref[...], jnp.concatenate(cols, 1))
                sr = [spec[:length, j * length : (j + 1) * length] for j in range(2)]
                si = [spec[length:, j * length : (j + 1) * length] for j in range(2)]
                real.append(kr[0] * sr[0] - ki[0] * si[0] + (kr[1] * sr[1] - ki[1] * si[1]))
                imag.append(kr[0] * si[0] + ki[0] * sr[0] + (kr[1] * si[1] + ki[1] * sr[1]))
            product = jnp.concatenate(
                [jnp.concatenate(real, 1).astype(bf16), jnp.concatenate(imag, 1).astype(bf16)], 0
            )
            done = dot(ix_ref[...], product).astype(bf16)
            flat = []
            for r in range(rotations):
                at = slice(r * length, (r + 1) * length)
                flat.append(jnp.concatenate([done[:length, at], done[length:, at]], 1))
            planes = dot(jnp.concatenate(flat, 0), iy_ref[...])
            for p in range(2):
                hold[p, pl.ds(k * rows, rows), :] = planes[:, p * length : (p + 1) * length]

    def collect(c, ref, first):
        @pl.loop(0, half, unroll=4)
        def _(x):
            for r in range(rotations):
                at = pl.ds(r * length + first + x, SUB, stride=rows)
                ref[c, r, x] = jnp.concatenate([hold[0, at, :], hold[1, at, :]], 0).astype(bf16)

    def open_chunk(c):
        for d in range(2):
            ring_send(d, c, 0)
        pair(0, c, 0, core).start()

    join(0)
    open_chunk(0)

    @pl.loop(0, chunks + 2)
    def _(i):
        c1, c2 = i - 1, i - 2

        @pl.when((c1 >= 0) & (c1 < chunks))
        def _():
            arrived(c1, 1)

        @pl.when(i + 1 < chunks)
        def _():
            join(i + 1)

        @pl.when(i == 2)
        def _():
            load.wait()

        @pl.when(c2 >= 0)
        def _():
            def act(d):
                ring_wait(d, c2, far_step)
                pair(d, c2, far_step + 1, core).start()

            for_far(c2, act)
            pair(0, c2, 0, 1 - core).wait_recv()
            for t in range(1, far_step + 1):
                for d in range(2):
                    pair(d, c2, t, 1 - core).wait_recv()
            for_far(c2, lambda d: pair(d, c2, far_step + 1, 1 - core).wait_recv())
            compute(c2, 0)

        @pl.when(i < chunks)
        def _():
            arrived(i, 0)

        @pl.when((c1 >= 0) & (c1 < chunks))
        def _():
            arrived(c1, 2)
            for_far(c1, lambda d: ring_send(d, c1, far_step))

        @pl.when(i + 1 < chunks)
        def _():
            open_chunk(i + 1)

        @pl.when(c2 >= 0)
        def _():
            compute(c2, SUB // 2)
            collect(c2, send, half)
            collect(c2, mine_ref, 0)
            for q in range(half // TILE):
                slab_copy(c2, q).start()

    @pl.loop(0, chunks)
    def _(c):
        for t in range(far_step):
            for d in range(2):
                ring(d, c, t, device(origin(d, t), core)).wait_send()
                pair(d, c, t + 1, core).wait_send()
        pair(0, c, 0, core).wait_send()

        def act(d):
            ring(d, c, far_step, device(origin(d, far_step), core)).wait_send()
            pair(d, c, far_step + 1, core).wait_send()

        for_far(c, act)
        swap(c).wait_send()

    @pl.loop(0, half // TILE)
    def _(q):
        @pl.loop(0, chunks)
        def _(c):
            slab_copy(c, q).wait_send()
            slab_copy(c, q).wait_recv()

        @pl.loop(0, TILE, unroll=2)
        def _(x):
            cols = []
            for r in range(rotations):
                tiles = [
                    ref[t, r, q * TILE + x] for ref in (mine_ref, far_ref) for t in range(chunks)
                ]
                cols.append(jnp.concatenate(tiles, 0))
            scores = dot(mz_ref[...], jnp.concatenate(cols, 1))
            best = scores[:, :length]
            for r in range(1, rotations):
                best = jnp.maximum(best, scores[:, r * length : (r + 1) * length])
            hold[0, pl.ds(x * length, length), :] = best

        @pl.loop(0, length, unroll=4)
        def _(z):
            at = pl.ds(pl.multiple_of(q * TILE, TILE), TILE)
            out_ref[z, at, :] = hold[0, pl.ds(z, TILE, stride=length), :].astype(bf16)


def quick_body(groups, ligand_grids, receptor_kernel):
    rotations, channels, depth, width, length = ligand_grids.shape
    pairs = channels // 2
    grids = rotations * pairs
    half = length // 2
    block = width // groups
    side = 2 * length
    consts = matrices(length, groups)
    own = lax.axis_index("slab")
    fz, fx, ix, mz = [
        lax.dynamic_index_in_dim(jnp.asarray(m).astype(bf16), own, 0, keepdims=False) for m in consts[:4]
    ]
    fy, iy = [jnp.asarray(m).astype(bf16) for m in consts[4:]]
    whole = pl.BlockSpec(memory_space=pltpu.VMEM)

    blocks = pl.pallas_call(
        functools.partial(split_kernel, rotations, pairs, depth, width, block),
        out_shape=jax.ShapeDtypeStruct((groups, block, grids, 2 * depth, length), bf16),
        in_specs=[whole],
        out_specs=whole,
    )(ligand_grids.reshape(-1, length))
    lines = lax.all_to_all(blocks, "grp", split_axis=0, concat_axis=0, tiled=True)
    shape = jax.ShapeDtypeStruct((half, grids, 2 * block, length), bf16)
    mine, other = pl.pallas_call(
        functools.partial(zy_kernel, rotations, groups, block, length),
        out_shape=[shape, shape],
        in_specs=[whole] * 3,
        out_specs=[whole] * 2,
        scratch_shapes=[pltpu.VMEM((2 * block * grids * length, length), f32)],
    )(fz, fy, lines)

    rec = receptor_kernel[0]
    chunks = half // SUB
    hops = groups // 4
    part = jax.ShapeDtypeStruct((chunks, rotations, half, TILE, length), bf16)
    dma = pltpu.SemaphoreType.DMA
    best = pl.pallas_call(
        functools.partial(score_kernel, rotations, groups, length, chunks),
        out_shape=jax.ShapeDtypeStruct((length, half, length), bf16),
        in_specs=[whole] * 4 + [pl.BlockSpec(memory_space=pl.ANY), whole, whole],
        out_specs=whole,
        scratch_shapes=[
            pltpu.VMEM(part.shape, bf16),
            pltpu.VMEM(part.shape, bf16),
            pltpu.VMEM((groups, half, grids, TILE, length), bf16),
            pltpu.VMEM(other.shape, bf16),
            pltpu.VMEM(rec.shape, bf16),
            pltpu.VMEM(part.shape, bf16),
            pltpu.VMEM((2, SUB * rotations * length, length), f32),
            dma,
            dma((chunks,)),
            dma((chunks,)),
            dma((2, chunks, hops)),
            dma((2, chunks, hops)),
            dma((2, chunks, hops + 1)),
            dma((2, chunks, hops + 1)),
            dma((chunks, half // TILE)),
            dma((chunks, half // TILE)),
        ],
        compiler_params=pltpu.CompilerParams(
            collective_id=0, has_side_effects=True, vmem_limit_bytes=60 * 2**20
        ),
    )(fx, ix, iy, mz, rec, mine, other)

    return best[None]


def choose(groups, slabs, ligand_grids, receptor_kernel):
    rotations, channels, depth, width, length = ligand_grids.shape
    fits = (
        slabs == 2
        and channels == 4
        and rotations == 2
        and depth == SUB
        and width % groups == 0
        and 4 * (width // groups) == TILE
        and length % 128 == 0
        and (length // 2) % SUB == 0
        and groups == 4 * 4
        and (length // 2) % TILE == 0
    )
    if fits:
        return quick_body(groups, ligand_grids, receptor_kernel)
    return body(ligand_grids, receptor_kernel)


def solution(mesh):
    return jax.shard_map(
        functools.partial(choose, mesh.shape["grp"], mesh.shape["slab"]),
        mesh=mesh,
        in_specs=(P(None, None, "grp", "slab", None), P("grp", None, None, "slab", None, None)),
        out_specs=P("grp", None, "slab", None),
        check_vma=False,
    )
```

profile of v0, /device:TPU:0, one launch (start us, length us, event | category | flops | bytes accessed | tf_op | source)
XLA Modules:
  0.0 183.0 jit_solution(3098156064280923621)
XLA Ops:
  0.0 0.0 copy-start.4
  0.0 0.0 copy-start.3
  0.0 0.0 copy-start.1
  0.0 0.0 copy-start.2
  0.0 5.1 %shard_map.82 = bf16[16,4,4,16,128]{4,3,2,1,0:T(8,128)(2,1)} custom-call(f32[4096,128]{1,0:T(8,128)} %bitcast.13), custom_call_target="tpu_custom_call" | custom-call | tf_op jit(solution)/shard_map/pallas_call | solution.py:428
  5.1 7.4 %all-to-all-start = ((bf16[16,4,4,16,128]{4,3,2,1,0:T(8,128)(2,1)}), bf16[16,4,4,16,128]{4,3,2,1,0:T(8,128)(2,1)S(1)}, u32[]{:S(2)}, u32[]{:S(2)}) async-start(bf16[16,4,4,16,128]{4,3,2,1,0:T(8,128)(2,1)} %shard_map.82), calls=%async_computation | async-start | bytes 2097152 | tf_op jit(solution)/shard_map/all_to_all | solution.py:434
  12.5 0.0 copy-done.4
  12.5 0.6 dynamic-slice_bitcast_fusion.3.mz_ref
  13.2 0.0 copy-done.3
  13.2 0.7 dynamic-slice_bitcast_fusion.2.fx_ref
  13.8 0.0 copy-done.1
  13.8 0.0 copy-done.2
  13.8 0.7 dynamic-slice_bitcast_fusion
  14.6 20.8 %all-to-all-done.in_ref = bf16[16,4,4,16,128]{4,3,2,1,0:T(8,128)(2,1)S(1)} async-done(((bf16[16,4,4,16,128]{4,3,2,1,0:T(8,128)(2,1)}), bf16[16,4,4,16,128]{4,3,2,1,0:T(8,128)(2,1)S(1)}, u32[]{:S(2)}, u32[]{:S(2)}) %all-to-all-start) | async-done | bytes 1048608 | tf_op jit(solution)/shard_map/all_to_all | solution.py:434
  35.4 0.0 copy-start
  35.4 1.0 copy-done
  36.4 6.0 %shard_map.83 = (bf16[64,4,8,128]{3,2,1,0:T(8,128)(2,1)}, bf16[64,4,8,128]{3,2,1,0:T(8,128)(2,1)}) custom-call(bf16[256,256]{1,0:T(8,128)(2,1)} %get-tuple-element.9.fz_ref, bf16[256,256]{1,0:T(8,128)(2,1)} %constant.43.fy_ref, bf16[16,4,4,16,128]{4,3,2,1,0:T(8,128)(2,1)} %copy-done), custom_call_target="tpu_custom_call" | custom-call | tf_op jit(solution)/shard_map/pallas_call | solution.py:436
  42.4 137.5 %shard_map.84 = bf16[128,64,128]{2,1,0:T(8,128)(2,1)} custom-call(bf16[256,256]{1,0:T(8,128)(2,1)} %dynamic-slice_bitcast_fusion.2.fx_ref, bf16[256,256]{1,0:T(8,128)(2,1)} %get-tuple-element.10.ix_ref, bf16[256,256]{1,0:T(8,128)(2,1)} %constant.40.iy_ref, bf16[128,256]{1,0:T(8,128)(2,1)} %dynamic-slice_bitcast_fusion.3.mz_ref, ...), custom_call_target="tpu_custom_call" | custom-call | tf_op jit(solution)/shard_map/pallas_call | solution.py:449
  179.9 3.1 %copy.10 = bf16[1,128,64,128]{3,2,1,0:T(8,128)(2,1)} copy(bf16[1,128,64,128]{3,2,1,0:T(8,128)(2,1)} %bitcast.12) | data formatting | bytes 4194304
Async XLA Ops:
  0.0 12.5 %copy-start.4 = (bf16[2,128,256]{2,1,0:T(8,128)(2,1)S(1)}, bf16[2,128,256]{2,1,0:T(8,128)(2,1)}, u32[]{:S(2)}) copy-start(bf16[2,128,256]{2,1,0:T(8,128)(2,1)} %constant.41) | copy-start | bytes 393220
  0.0 13.2 %copy-start.3 = (bf16[2,256,256]{2,1,0:T(8,128)(2,1)S(1)}, bf16[2,256,256]{2,1,0:T(8,128)(2,1)}, u32[]{:S(2)}) copy-start(bf16[2,256,256]{2,1,0:T(8,128)(2,1)} %constant.38) | copy-start | bytes 786436
  0.0 13.8 %copy-start.1 = (bf16[2,256,256]{2,1,0:T(8,128)(2,1)S(1)}, bf16[2,256,256]{2,1,0:T(8,128)(2,1)}, u32[]{:S(2)}) copy-start(bf16[2,256,256]{2,1,0:T(8,128)(2,1)} %constant.42) | copy-start | bytes 786436
  0.0 13.8 %copy-start.2 = (bf16[2,256,256]{2,1,0:T(8,128)(2,1)S(1)}, bf16[2,256,256]{2,1,0:T(8,128)(2,1)}, u32[]{:S(2)}) copy-start(bf16[2,256,256]{2,1,0:T(8,128)(2,1)} %constant.39) | copy-start | bytes 786436
  5.1 30.3 %all-to-all-start = ((bf16[16,4,4,16,128]{4,3,2,1,0:T(8,128)(2,1)}), bf16[16,4,4,16,128]{4,3,2,1,0:T(8,128)(2,1)S(1)}, u32[]{:S(2)}, u32[]{:S(2)}) async-start(bf16[16,4,4,16,128]{4,3,2,1,0:T(8,128)(2,1)} %shard_map.82), calls=%async_computation | async-start | bytes 2097152 | tf_op jit(solution)/shard_map/all_to_all | solution.py:434
  35.4 1.0 copy-start
where the time goes:
time: 183 us
  Pallas kernels  149 us (81%)
  waiting for transfers between devices  20.8 us (11%)
  starting transfers between devices  7.4 us (4%)
  local copies, waits for them, and re-layouts  6.11 us (3%)
    pallas_call x1, Pallas kernels, quick_body(): pl.pallas_call(functools.partial(score_kernel, rotations, groups, length,...  138 us
    all_to_all x1, waiting for transfers between devices, quick_body(): lax.all_to_all(blocks, 'grp', split_axis=0, concat_axis=0, tiled=True)  20.8 us
    all_to_all x1, starting transfers between devices, quick_body(): lax.all_to_all(blocks, 'grp', split_axis=0, concat_axis=0, tiled=True)  7.4 us
    pallas_call x1, Pallas kernels, quick_body(): pl.pallas_call(functools.partial(zy_kernel, rotations, groups, block, len...  6.03 us
    pallas_call x1, Pallas kernels, quick_body(): pl.pallas_call(functools.partial(split_kernel, rotations, pairs, depth, w...  5.09 us
    unnamed x11, local copies, waits for them, and re-layouts  4.06 us
  transfers between devices with their start and end apart: 1, of which 1 were waited for; matrix products, arithmetic and copies ran while one was open for 1% of the time, Pallas kernels for 0%

commit v1 on v0

--- a/solution.py
+++ b/solution.py
@@ -81,6 +81,7 @@
 
 TILE = 16
 SUB = 8
+MOVED = 8
 f32 = jnp.float32
 bf16 = jnp.bfloat16
 
@@ -95,84 +96,156 @@
     return forward, inverse
 
 
-def matrices(length, groups):
+def frequencies(length, moved, own):
+    half = length // 2
+    base, across = own * half, (1 - own) * half
+    single = [base] + [base + n for n in range(moved + 1, half - moved)]
+    kept = [base + half - moved + n for n in range(moved)]
+    taken = [across + moved - n for n in range(moved)]
+    return single, kept, taken
+
+
+def matrices(length, groups, moved):
     forward, inverse = waves(length)
     half, side = length // 2, 2 * length
-    block = half // groups
-    fz, fx, ix, mz = [], [], [], []
+    chips = groups // 2
+    orders, lasting = [], []
     for own in range(2):
+        single, kept, taken = frequencies(length, moved, own)
+        orders.append(single + [k for both in zip(kept, taken) for k in both])
+        lasting.append(single + kept)
+    fz, ix, mz = [], [], []
+    for own in range(2):
+        order = np.array(orders[own] + orders[1 - own])
+        fz.append(forward[:, :, order].transpose(0, 2, 1, 3).reshape(side, side))
         order = (np.arange(length) + own * half) % length
-        by_cell = forward[:, :, order].reshape(2, 2, length, groups, length // groups)
-        fz.append(by_cell.transpose(0, 2, 3, 1, 4).reshape(side, side))
-        cells = forward[:, :, :, order].reshape(2, 2, length, 2, groups, block)
-        fx.append(cells.transpose(0, 2, 4, 3, 1, 5).reshape(side, side))
         ix.append(inverse[:, :, order].transpose(0, 2, 1, 3).reshape(side, side))
-        lines = inverse[0][:, :, order].reshape(2, length, length // SUB, SUB)
-        mz.append(lines.transpose(1, 2, 0, 3).reshape(length, side))
+        order = np.array(lasting[own] + lasting[1 - own])
+        lines = inverse[0][:, :, order].reshape(2, length, len(order) // SUB, SUB)
+        mz.append(lines.transpose(1, 2, 0, 3).reshape(length, 2 * len(order)))
+    cells = forward.reshape(2, 2, length, 2, chips, half // chips)
+    fx = cells.transpose(0, 2, 4, 3, 1, 5).reshape(side, side)
     fy = forward.transpose(1, 3, 0, 2).reshape(side, side)
     iy = inverse.transpose(1, 3, 0, 2).reshape(side, side)
-    return [np.stack(m).astype(np.float32) for m in (fz, fx, ix, mz)] + [
-        fy.astype(np.float32),
-        iy.astype(np.float32),
-    ]
+    return [jnp.asarray(np.stack(m) if isinstance(m, list) else m).astype(bf16) for m in (fz, fy, fx, ix, iy, mz)]
 
 
 def dot(a, b):
     return jnp.dot(a, b, preferred_element_type=f32)
 
 
-def split_kernel(rotations, pairs, depth, width, block, lig_ref, out_ref):
-    @pl.loop(0, width)
-    def _(x):
-        for r in range(rotations):
-            for j in range(pairs):
-                parts = []
-                for q in range(2):
-                    first = ((r * pairs + j) * 2 + q) * depth * width
-                    parts.append(lig_ref[pl.ds(first + x, depth, stride=width), :])
-                out_ref[x // block, x % block, r * pairs + j] = jnp.concatenate(parts, 0).astype(bf16)
-
-
-def zy_kernel(rotations, groups, block, length, fz_ref, fy_ref, in_ref, mine_ref, other_ref, hold):
-    fz = fz_ref[...]
-    fy = fy_ref[...]
-    grids = 2 * rotations
-
-    @pl.loop(0, block)
-    def _(x):
-        for r in range(rotations):
-            cols = [
-                jnp.concatenate([in_ref[g, x, 2 * r + j] for g in range(groups)], 0) for j in range(2)
-            ]
-            lines = dot(fz, jnp.concatenate(cols, 1)).astype(bf16)
-            rows = []
-            for j in range(2):
-                at = slice(j * length, (j + 1) * length)
-                rows.append(jnp.concatenate([lines[:length, at], lines[length:, at]], 1))
-            plane = dot(jnp.concatenate(rows, 0), fy)
-            for p in range(2):
-                start = ((p * block + x) * grids + 2 * r) * length
-                hold[pl.ds(start, 2 * length), :] = plane[:, p * length : (p + 1) * length]
-
-    stride = grids * length
-    half = length // 2
-
-    @pl.loop(0, half, unroll=2)
-    def _(k):
-        for i in range(grids):
-            mine_ref[k, i] = hold[pl.ds(i * length + k, 2 * block, stride=stride), :].astype(bf16)
-            other_ref[k, i] = hold[pl.ds(i * length + half + k, 2 * block, stride=stride), :].astype(
-                bf16
-            )
-
-
-def score_kernel(
-    rotations, groups, length, chunks, fx_ref, ix_ref, iy_ref, mz_ref, rec_ref, near_ref, swap_ref, out_ref,
-    mine_ref, far_ref, held, came, rec, send, hold, rec_sem, swap_out, swap_in, ring_out, ring_in, pair_out, pair_in, slab_out, slab_in,
+def front_kernel(
+    moved, groups, lig_ref, rec_ref, fy_ref, fz_ref, near_ref, swap_ref, give_ref,
+    blocks, lines, along, hold, line_out, line_in, own_sem, give_out, give_in,
 ):
     me = lax.axis_index("grp")
     slab = lax.axis_index("slab")
     core = lax.rem(me, 2)
+    chip = lax.div(me, 2)
+    rotations, channels, depth, width, length = lig_ref.shape
+    pairs = channels // 2
+    chips = groups // 2
+    block = width // chips
+    rows = depth * block
+    half = length // 2
+    MESH = pl.DeviceIdType.MESH
+    across = {"grp": me, "slab": 1 - slab}
+    barrier = pltpu.get_barrier_semaphore()
+    pl.semaphore_signal(barrier, inc=1, device_id=across, device_id_type=MESH)
+
+    @pl.loop(1, groups)
+    def _(o):
+        to = {"grp": lax.rem(me + o, groups), "slab": slab}
+        pl.semaphore_signal(barrier, inc=1, device_id=to, device_id_type=MESH)
+
+    @pl.loop(0, chips)
+    def _(b):
+        for r in range(rotations):
+            for j in range(pairs):
+                for q in range(2):
+                    piece = lig_ref[r, 2 * j + q, :, pl.ds(pl.multiple_of(b * block, block), block), :]
+                    blocks[b, r, j, q] = piece.reshape(rows, length).astype(bf16)
+
+    pl.semaphore_wait(barrier, groups)
+
+    def give(p, j):
+        return pltpu.make_async_remote_copy(
+            src_ref=rec_ref.at[p, j, pl.ds(1, moved)], dst_ref=give_ref.at[p, j],
+            send_sem=give_out.at[p, j], recv_sem=give_in.at[p, j],
+            device_id=across, device_id_type=MESH,
+        )
+
+    def line(o, j):
+        to = lax.rem(me + o, groups)
+        return pltpu.make_async_remote_copy(
+            src_ref=blocks.at[lax.div(to, 2), lax.rem(to, 2), j], dst_ref=lines.at[j, me],
+            send_sem=line_out.at[j, o], recv_sem=line_in.at[j, o],
+            device_id={"grp": to, "slab": slab}, device_id_type=MESH,
+        )
+
+    def stay(j):
+        return pltpu.make_async_copy(blocks.at[chip, core, j], lines.at[j, me], own_sem.at[j])
+
+    for j in range(pairs):
+        @pl.loop(1, groups)
+        def _(o):
+            line(o, j).start()
+
+        stay(j).start()
+    if moved:
+        for p in range(2):
+            for j in range(pairs):
+                give(p, j).start()
+
+    def along_y(j, g):
+        plane = dot(jnp.concatenate([lines[j, g, 0], lines[j, g, 1]], 1), fy_ref[...])
+        for p in range(2):
+            at = pl.ds(pl.multiple_of(g * rows, rows), rows)
+            along[p, at, :] = plane[:, p * length : (p + 1) * length]
+
+    for j in range(pairs):
+        stay(j).wait()
+        along_y(j, me)
+
+        @pl.loop(1, groups)
+        def _(o):
+            line(o, j).wait_recv()
+            along_y(j, lax.rem(me + groups - o, groups))
+
+        @pl.loop(0, block)
+        def _(x):
+            parts = [along[p, pl.ds(x, length, stride=block), :].astype(bf16) for p in range(2)]
+            found = dot(fz_ref[slab], jnp.concatenate(parts, 0))
+            for p in range(2):
+                at = pl.ds(pl.multiple_of((p * block + x) * length, length), length)
+                hold[at, :] = found[p * length : (p + 1) * length, :]
+
+        @pl.loop(0, half, unroll=4)
+        def _(k):
+            near_ref[k, j] = hold[pl.ds(k, 2 * block, stride=length), :].astype(bf16)
+            swap_ref[k, j] = hold[pl.ds(half + k, 2 * block, stride=length), :].astype(bf16)
+
+    for j in range(pairs):
+        @pl.loop(1, groups)
+        def _(o):
+            line(o, j).wait_send()
+
+    if moved:
+        for p in range(2):
+            for j in range(pairs):
+                give(p, j).wait()
+
+
+def score_kernel(
+    rotations, groups, length, chunks, moved, fx_ref, ix_ref, iy_ref, mz_ref, rec_ref, give_ref, near_ref, swap_ref, out_ref,
+    mine_ref, far_ref, held, rec, send, hold, rec_sem, near_sem, swap_out, swap_in, ring_out, ring_in, pair_out, pair_in, slab_out, slab_in,
+):
+    me = lax.axis_index("grp")
+    slab = lax.axis_index("slab")
+    core = lax.rem(me, 2)
+    half = length // 2
+    single = (half - 2 * moved) // SUB
+    lasting = single + moved // SUB
     height = groups // 4
     around = groups // 2
     row = me // 4
@@ -191,8 +264,21 @@
 
     across = {"grp": me, "slab": 1 - slab}
     MESH = pl.DeviceIdType.MESH
-    load = pltpu.make_async_copy(rec_ref, rec, rec_sem)
-    load.start()
+    rest = half - 1 - moved
+    loads = [
+        pltpu.make_async_copy(from_ref, rec.at[:, :, pl.ds(at, many)], rec_sem.at[n])
+        for n, (from_ref, at, many) in enumerate(
+            [
+                (rec_ref.at[:, :, pl.ds(0, 1)], 0, 1),
+                (rec_ref.at[:, :, pl.ds(moved + 1, rest)], moved + 1, rest),
+            ]
+            + [(give_ref, 1, moved)] * (moved > 0)
+        )
+    ]
+    place_own = pltpu.make_async_copy(near_ref, held.at[me, slab], near_sem)
+    place_own.start()
+    for load in loads:
+        load.start()
     barrier = pltpu.get_barrier_semaphore()
     for to in (place(beside[0]), place(beside[1]), place(partner), across):
         pl.semaphore_signal(barrier, inc=1, device_id=to, device_id_type=MESH)
@@ -201,7 +287,7 @@
     def swap(c):
         at = pl.ds(c * SUB, SUB)
         return pltpu.make_async_remote_copy(
-            src_ref=swap_ref.at[at], dst_ref=came.at[at],
+            src_ref=swap_ref.at[at], dst_ref=held.at[me, slab, at],
             send_sem=swap_out.at[c], recv_sem=swap_in.at[c],
             device_id=across, device_id_type=MESH,
         )
@@ -213,18 +299,11 @@
     def join(c):
         swap(c).wait_recv()
 
-        @pl.loop(0, SUB)
-        def _(k):
-            z = c * SUB + k
-            for g in range(near_ref.shape[1]):
-                both = [near_ref[z, g].astype(f32), came[z, g].astype(f32)]
-                held[me, z, g] = jnp.concatenate(both, 0).astype(bf16)
-
     def origin(d, t):
         return spot - t if d == 0 else spot + t
 
     def part(slot, c):
-        return held.at[slot, pl.ds(c * SUB, SUB)]
+        return held.at[slot, :, pl.ds(c * SUB, SUB)]
 
     def ring(d, c, t, slot):
         return pltpu.make_async_remote_copy(
@@ -271,36 +350,61 @@
             pair(d, c, t + 1, core).start()
 
     rows = rotations * length
-    half = length // 2
-
-    def compute(c, first):
+    chips = groups // 2
+
+    def plane(z, slot):
+        kr = [rec[0, j, slot].astype(f32) for j in range(2)]
+        ki = [rec[1, j, slot].astype(f32) for j in range(2)]
+        real, imag = [], []
+        for r in range(rotations):
+            cols = [
+                jnp.concatenate([held[2 * b + r, s, z, j] for b in range(chips) for s in range(2)], 0)
+                for j in range(2)
+            ]
+            spec = dot(fx_ref[...], jnp.concatenate(cols, 1))
+            sr = [spec[:length, j * length : (j + 1) * length] for j in range(2)]
+            si = [spec[length:, j * length : (j + 1) * length] for j in range(2)]
+            real.append(kr[0] * sr[0] - ki[0] * si[0] + (kr[1] * sr[1] - ki[1] * si[1]))
+            imag.append(kr[0] * si[0] + ki[0] * sr[0] + (kr[1] * si[1] + ki[1] * sr[1]))
+        product = jnp.concatenate(
+            [jnp.concatenate(real, 1).astype(bf16), jnp.concatenate(imag, 1).astype(bf16)], 0
+        )
+        done = dot(ix_ref[slab], product).astype(bf16)
+        flat = []
+        for r in range(rotations):
+            at = slice(r * length, (r + 1) * length)
+            flat.append(jnp.concatenate([done[:length, at], done[length:, at]], 1))
+        return dot(jnp.concatenate(flat, 0), iy_ref[...])
+
+    def keep(k, parts):
+        for p in range(2):
+            hold[p, pl.ds(pl.multiple_of(k * rows, rows), rows), :] = parts[p]
+
+    def alone(c, first):
         @pl.loop(first, first + SUB // 2, unroll=2)
         def _(k):
             z = c * SUB + k
-            kr = [rec[0, j, z].astype(f32) for j in range(2)]
-            ki = [rec[1, j, z].astype(f32) for j in range(2)]
-            real, imag = [], []
-            for r in range(rotations):
-                cols = [
-                    jnp.concatenate([held[g, z, 2 * r + j] for g in range(groups)], 0)
-                    for j in range(2)
-                ]
-                spec = dot(fx_ref[...], jnp.concatenate(cols, 1))
-                sr = [spec[:length, j * length : (j + 1) * length] for j in range(2)]
-                si = [spec[length:, j * length : (j + 1) * length] for j in range(2)]
-                real.append(kr[0] * sr[0] - ki[0] * si[0] + (kr[1] * sr[1] - ki[1] * si[1]))
-                imag.append(kr[0] * si[0] + ki[0] * sr[0] + (kr[1] * si[1] + ki[1] * sr[1]))
-            product = jnp.concatenate(
-                [jnp.concatenate(real, 1).astype(bf16), jnp.concatenate(imag, 1).astype(bf16)], 0
-            )
-            done = dot(ix_ref[...], product).astype(bf16)
-            flat = []
-            for r in range(rotations):
-                at = slice(r * length, (r + 1) * length)
-                flat.append(jnp.concatenate([done[:length, at], done[length:, at]], 1))
-            planes = dot(jnp.concatenate(flat, 0), iy_ref[...])
-            for p in range(2):
-                hold[p, pl.ds(k * rows, rows), :] = planes[:, p * length : (p + 1) * length]
+            both = plane(z, jnp.where(z == 0, 0, z + moved))
+            keep(k, [both[:, :length], both[:, length:]])
+
+    def mirrored(c, first):
+        @pl.loop(0, SUB // 4)
+        def _(q):
+            z = c * SUB + first + 2 * q
+            n = lax.div(z - single * SUB, 2)
+            one = plane(z, half - moved + n)
+            two = plane(z + 1, moved - n)
+            keep(lax.rem(n, SUB), [one[:, :length] + two[:, :length], one[:, length:] - two[:, length:]])
+
+    def compute(c, first):
+        @pl.when(c < single)
+        def _():
+            alone(c, first)
+
+        if moved:
+            @pl.when(c >= single)
+            def _():
+                mirrored(c, first)
 
     def collect(c, ref, first):
         @pl.loop(0, half, unroll=4)
@@ -314,6 +418,7 @@
             ring_send(d, c, 0)
         pair(0, c, 0, core).start()
 
+    place_own.wait()
     join(0)
     open_chunk(0)
 
@@ -331,7 +436,8 @@
 
         @pl.when(i == 2)
         def _():
-            load.wait()
+            for load in loads:
+                load.wait()
 
         @pl.when(c2 >= 0)
         def _():
@@ -363,10 +469,15 @@
         @pl.when(c2 >= 0)
         def _():
             compute(c2, SUB // 2)
-            collect(c2, send, half)
-            collect(c2, mine_ref, 0)
-            for q in range(half // TILE):
-                slab_copy(c2, q).start()
+            over = c2 - single
+
+            @pl.when((over < 0) | (lax.rem(jnp.maximum(over, 0), 2) == 1))
+            def _():
+                c = jnp.where(over < 0, c2, single + lax.div(jnp.maximum(over, 0), 2))
+                collect(c, send, half)
+                collect(c, mine_ref, 0)
+                for q in range(half // TILE):
+                    slab_copy(c, q).start()
 
     @pl.loop(0, chunks)
     def _(c):
@@ -385,7 +496,7 @@
 
     @pl.loop(0, half // TILE)
     def _(q):
-        @pl.loop(0, chunks)
+        @pl.loop(0, lasting)
         def _(c):
             slab_copy(c, q).wait_send()
             slab_copy(c, q).wait_recv()
@@ -395,10 +506,10 @@
             cols = []
             for r in range(rotations):
                 tiles = [
-                    ref[t, r, q * TILE + x] for ref in (mine_ref, far_ref) for t in range(chunks)
+                    ref[t, r, q * TILE + x] for ref in (mine_ref, far_ref) for t in range(lasting)
                 ]
                 cols.append(jnp.concatenate(tiles, 0))
-            scores = dot(mz_ref[...], jnp.concatenate(cols, 1))
+            scores = dot(mz_ref[slab], jnp.concatenate(cols, 1))
             best = scores[:, :length]
             for r in range(1, rotations):
                 best = jnp.maximum(best, scores[:, r * length : (r + 1) * length])
@@ -413,52 +524,57 @@
 def quick_body(groups, ligand_grids, receptor_kernel):
     rotations, channels, depth, width, length = ligand_grids.shape
     pairs = channels // 2
-    grids = rotations * pairs
     half = length // 2
-    block = width // groups
-    side = 2 * length
-    consts = matrices(length, groups)
-    own = lax.axis_index("slab")
-    fz, fx, ix, mz = [
-        lax.dynamic_index_in_dim(jnp.asarray(m).astype(bf16), own, 0, keepdims=False) for m in consts[:4]
-    ]
-    fy, iy = [jnp.asarray(m).astype(bf16) for m in consts[4:]]
+    chips = groups // 2
+    block = width // chips
+    rows = depth * block
+    moved = MOVED
+    fz, fy, fx, ix, iy, mz = matrices(length, groups, moved)
     whole = pl.BlockSpec(memory_space=pltpu.VMEM)
-
-    blocks = pl.pallas_call(
-        functools.partial(split_kernel, rotations, pairs, depth, width, block),
-        out_shape=jax.ShapeDtypeStruct((groups, block, grids, 2 * depth, length), bf16),
-        in_specs=[whole],
-        out_specs=whole,
-    )(ligand_grids.reshape(-1, length))
-    lines = lax.all_to_all(blocks, "grp", split_axis=0, concat_axis=0, tiled=True)
-    shape = jax.ShapeDtypeStruct((half, grids, 2 * block, length), bf16)
-    mine, other = pl.pallas_call(
-        functools.partial(zy_kernel, rotations, groups, block, length),
-        out_shape=[shape, shape],
-        in_specs=[whole] * 3,
-        out_specs=[whole] * 2,
-        scratch_shapes=[pltpu.VMEM((2 * block * grids * length, length), f32)],
-    )(fz, fy, lines)
-
+    away = pl.BlockSpec(memory_space=pl.ANY)
+    dma = pltpu.SemaphoreType.DMA
     rec = receptor_kernel[0]
+
+    shape = jax.ShapeDtypeStruct((half, pairs, 2 * block, length), bf16)
+    given = jax.ShapeDtypeStruct((2, pairs, moved, length, length), bf16)
+    near, other, give = pl.pallas_call(
+        functools.partial(front_kernel, moved, groups),
+        out_shape=[shape, shape, given],
+        in_specs=[whole, away, whole, whole],
+        out_specs=[whole, whole, away],
+        scratch_shapes=[
+            pltpu.VMEM((chips, rotations, pairs, 2, rows, length), bf16),
+            pltpu.VMEM((pairs, groups, 2, rows, length), bf16),
+            pltpu.VMEM((2, block * length, length), f32),
+            pltpu.VMEM((2 * block * length, length), f32),
+            dma((pairs, groups)),
+            dma((pairs, groups)),
+            dma((pairs,)),
+            dma((2, pairs)),
+            dma((2, pairs)),
+        ],
+        compiler_params=pltpu.CompilerParams(
+            collective_id=1, has_side_effects=True, vmem_limit_bytes=24 * 2**20
+        ),
+    )(ligand_grids, rec, fy, fz)
+
     chunks = half // SUB
     hops = groups // 4
-    part = jax.ShapeDtypeStruct((chunks, rotations, half, TILE, length), bf16)
-    dma = pltpu.SemaphoreType.DMA
+    lasting = chunks - moved // SUB
+    part = (lasting, rotations, half, TILE, length)
     best = pl.pallas_call(
-        functools.partial(score_kernel, rotations, groups, length, chunks),
+        functools.partial(score_kernel, rotations, groups, length, chunks, moved),
         out_shape=jax.ShapeDtypeStruct((length, half, length), bf16),
-        in_specs=[whole] * 4 + [pl.BlockSpec(memory_space=pl.ANY), whole, whole],
+        in_specs=[whole] * 4 + [away] * 4,
         out_specs=whole,
         scratch_shapes=[
-            pltpu.VMEM(part.shape, bf16),
-            pltpu.VMEM(part.shape, bf16),
-            pltpu.VMEM((groups, half, grids, TILE, length), bf16),
-            pltpu.VMEM(other.shape, bf16),
+            pltpu.VMEM(part, bf16),
+            pltpu.VMEM(part, bf16),
+            pltpu.VMEM((groups, 2, half, pairs, TILE, length), bf16),
             pltpu.VMEM(rec.shape, bf16),
-            pltpu.VMEM(part.shape, bf16),
+            pltpu.VMEM(part, bf16),
             pltpu.VMEM((2, SUB * rotations * length, length), f32),
+            dma((3,)),
             dma,
             dma((chunks,)),
             dma((chunks,)),
@@ -466,13 +582,13 @@
             dma((2, chunks, hops)),
             dma((2, chunks, hops + 1)),
             dma((2, chunks, hops + 1)),
-            dma((chunks, half // TILE)),
-            dma((chunks, half // TILE)),
+            dma((lasting, half // TILE)),
+            dma((lasting, half // TILE)),
         ],
         compiler_params=pltpu.CompilerParams(
             collective_id=0, has_side_effects=True, vmem_limit_bytes=60 * 2**20
         ),
-    )(fx, ix, iy, mz, rec, mine, other)
+    )(fx, ix, iy, mz, rec, give, near, other)
 
     return best[None]
 
@@ -484,8 +600,9 @@
         and channels == 4
         and rotations == 2
         and depth == SUB
-        and width % groups == 0
-        and 4 * (width // groups) == TILE
+        and depth * groups == length
+        and 2 * width == length
+        and width // (groups // 2) == SUB
         and length % 128 == 0
         and (length // 2) % SUB == 0
         and groups == 4 * 4

time: 183 us -> 172 us (0.940)
  waiting for transfers between devices: 20.8 us -> 0 us
  Pallas kernels: 149 us -> 159 us
  starting transfers between devices: 7.4 us -> 0 us
  local copies, waits for them, and re-layouts: 6.11 us -> 12.5 us
    pallas_call x2 -> x1, Pallas kernels: 11.1 us -> 32 us  [quick_body(): pl.pallas_call(functools.partial(front_kernel, moved, groups), out_shape=...]
    all_to_all x1 -> x0, waiting for transfers between devices: 20.8 us -> none  [quick_body(): lax.all_to_all(blocks, 'grp', split_axis=0, concat_axis=0, tiled=True)]
    pallas_call x1, Pallas kernels: 138 us -> 127 us  [quick_body(): pl.pallas_call(functools.partial(score_kernel, rotations, groups, length,...]
    unnamed x11 -> x15, local copies, waits for them, and re-layouts: 4.06 us -> 12.5 us
    all_to_all x1 -> x0, starting transfers between devices: 7.4 us -> none  [quick_body(): lax.all_to_all(blocks, 'grp', split_axis=0, concat_axis=0, tiled=True)]
    squeeze x3 -> x0, local copies, waits for them, and re-layouts: 2.04 us -> none  [quick_body(): lax.dynamic_index_in_dim(jnp.asarray(m).astype(bf16), own, 0, keepdims=Fa...]
  transfers between devices with their start and end apart: 1 -> 0, of which waited for: 1 -> 0; matrix products, arithmetic and copies ran while one was open for 1% -> 0% of each run, Pallas kernels for 0% -> 0%
where the time goes in v1:
time: 172 us; the launch traced here: 171 us
  Pallas kernels  159 us (92%)
  local copies, waits for them, and re-layouts  12.5 us (7%)
    pallas_call x1, Pallas kernels, quick_body(): pl.pallas_call(functools.partial(score_kernel, rotations, groups, length,...  127 us
    pallas_call x1, Pallas kernels, quick_body(): pl.pallas_call(functools.partial(front_kernel, moved, groups), out_shape=...  32 us
    unnamed x15, local copies, waits for them, and re-layouts  12.5 us

profile of v1, /device:TPU:0, one launch (start us, length us, event | category | flops | bytes accessed | tf_op | source)
XLA Modules:
  0.0 171.0 jit_solution(10978042174018181222)
XLA Ops:
  0.0 0.0 copy-start
  0.0 3.4 %copy-done = bf16[1,2,2,64,128,128]{5,4,3,2,1,0:T(8,128)(2,1)S(1)} copy-done((bf16[1,2,2,64,128,128]{5,4,3,2,1,0:T(8,128)(2,1)S(1)}, bf16[1,2,2,64,128,128]{5,4,3,2,1,0:T(8,128)(2,1)}, u32[]{:S(2)}) %copy-start) | copy-done | bytes 8388632
  3.4 0.0 copy-start.1
  3.4 1.6 copy-done.1
  5.0 0.0 copy-start.5
  5.0 0.9 copy-done.5
  5.9 0.0 copy-start.6
  5.9 0.9 copy-done.6
  6.8 32.0 %shard_map.82 = (bf16[64,2,16,128]{3,2,1,0:T(8,128)(2,1)S(1)}, bf16[64,2,16,128]{3,2,1,0:T(8,128)(2,1)S(1)}, bf16[2,2,8,128,128]{4,3,2,1,0:T(8,128)(2,1)S(1)}) custom-call(f32[2,4,8,64,128]{4,3,2,1,0:T(8,128)S(1)} %copy-done.1, bf16[2,2,64,128,128]{4,3,2,1,0:T(8,128)(2,1)S(1)} %bitcast.3, bf16[256,256]{1,0:T(8,128)(2,1)S(1)} %copy-done.6, ...), custom_call_target="tpu_custom_call" | custom-call | tf_op jit(solution)/shard_map/pallas_call | solution.py:540
  38.8 0.0 copy-start.2
  38.8 1.0 copy-done.2
  39.8 0.0 copy-start.3
  39.8 0.8 copy-done.3
  40.6 0.0 copy-start.4
  40.6 0.8 copy-done.4
  41.4 126.5 %shard_map.83 = bf16[128,64,128]{2,1,0:T(8,128)(2,1)} custom-call(bf16[256,256]{1,0:T(8,128)(2,1)} %constant.20.fx_ref, bf16[2,256,256]{2,1,0:T(8,128)(2,1)} %constant.21.ix_ref, bf16[256,256]{1,0:T(8,128)(2,1)} %constant.22.iy_ref, bf16[2,128,224]{2,1,0:T(8,128)(2,1)} %constant.23.mz_ref, bf16[2,2,64,128,128]{4,3,2,1,0:T(8,128)(2,1)} %bitcast.2, ...), custom_call_target="tpu_custom_call" | custom-call | tf_op jit(solution)/shard_map/pallas_call | solution.py:565
  167.9 3.1 %copy.10 = bf16[1,128,64,128]{3,2,1,0:T(8,128)(2,1)} copy(bf16[1,128,64,128]{3,2,1,0:T(8,128)(2,1)} %bitcast.4) | data formatting | bytes 4194304
Async XLA Ops:
  0.0 3.4 %copy-start = (bf16[1,2,2,64,128,128]{5,4,3,2,1,0:T(8,128)(2,1)S(1)}, bf16[1,2,2,64,128,128]{5,4,3,2,1,0:T(8,128)(2,1)}, u32[]{:S(2)}) copy-start(bf16[1,2,2,64,128,128]{5,4,3,2,1,0:T(8,128)(2,1)} %param.9) | copy-start | bytes 25165828
  3.4 1.6 copy-start.1
  5.0 0.9 copy-start.5
  5.9 0.9 copy-start.6
  38.8 1.0 copy-start.2
  39.8 0.8 copy-start.3
  40.6 0.8 copy-start.4

commit v2 on v1

--- a/solution.py
+++ b/solution.py
@@ -134,9 +134,11 @@
     return jnp.dot(a, b, preferred_element_type=f32)
 
 
-def front_kernel(
-    moved, groups, lig_ref, rec_ref, fy_ref, fz_ref, near_ref, swap_ref, give_ref,
-    blocks, lines, along, hold, line_out, line_in, own_sem, give_out, give_in,
+def dock_kernel(
+    groups, moved, fz_ref, fy_ref, fx_ref, ix_ref, iy_ref, mz_ref, lig_ref, rec_ref, out_ref,
+    lig, blocks, lines, along, other, held, rec, mine, far, send, hold,
+    lig_sem, rec_sem, own_sem, line_out, line_in, give_out, give_in,
+    swap_out, swap_in, ring_out, ring_in, pair_out, pair_in, slab_out, slab_in,
 ):
     me = lax.axis_index("grp")
     slab = lax.axis_index("slab")
@@ -146,168 +148,155 @@
     pairs = channels // 2
     chips = groups // 2
     block = width // chips
-    rows = depth * block
+    lot = depth * block
     half = length // 2
+    chunks = half // SUB
+    single = (half - 2 * moved) // SUB
+    lasting = single + moved // SUB
+    rows = rotations * length
+    height = groups // 4
+    around = groups // 2
+    row = lax.div(me, 4)
+    column = lax.rem(chip, 2)
+    spot = jnp.where(column == 0, row, around - 1 - row)
+    far_step = around // 2 - 1
     MESH = pl.DeviceIdType.MESH
+
+    def device(at, which):
+        at = lax.rem(at + around, around)
+        return jnp.where(at < height, at * 4, (around - 1 - at) * 4 + 2) + which
+
+    def place(to):
+        return {"grp": to, "slab": slab}
+
+    def turned(by):
+        return lax.rem(me + groups + by, groups)
+
+    beside = (device(spot + 1, core), device(spot - 1, core))
+    partner = device(spot, 1 - core)
     across = {"grp": me, "slab": 1 - slab}
+
+    lig_loads = [
+        pltpu.make_async_copy(lig_ref.at[:, pl.ds(2 * j, 2)], lig.at[:, pl.ds(2 * j, 2)], lig_sem.at[j])
+        for j in range(pairs)
+    ]
+    rest = half - 1 - moved
+    rec_loads = [
+        pltpu.make_async_copy(
+            rec_ref.at[:, :, pl.ds(at, many)], rec.at[:, :, pl.ds(at, many)], rec_sem.at[n]
+        )
+        for n, (at, many) in enumerate([(0, 1), (moved + 1, rest)])
+    ]
+    for load in lig_loads:
+        load.start()
+    for load in rec_loads:
+        load.start()
+
     barrier = pltpu.get_barrier_semaphore()
     pl.semaphore_signal(barrier, inc=1, device_id=across, device_id_type=MESH)
 
     @pl.loop(1, groups)
     def _(o):
-        to = {"grp": lax.rem(me + o, groups), "slab": slab}
-        pl.semaphore_signal(barrier, inc=1, device_id=to, device_id_type=MESH)
-
-    @pl.loop(0, chips)
-    def _(b):
-        for r in range(rotations):
-            for j in range(pairs):
-                for q in range(2):
-                    piece = lig_ref[r, 2 * j + q, :, pl.ds(pl.multiple_of(b * block, block), block), :]
-                    blocks[b, r, j, q] = piece.reshape(rows, length).astype(bf16)
-
-    pl.semaphore_wait(barrier, groups)
+        pl.semaphore_signal(barrier, inc=1, device_id=place(turned(o)), device_id_type=MESH)
 
     def give(p, j):
+        at = pl.ds(1, moved)
         return pltpu.make_async_remote_copy(
-            src_ref=rec_ref.at[p, j, pl.ds(1, moved)], dst_ref=give_ref.at[p, j],
+            src_ref=rec_ref.at[p, j, at], dst_ref=rec.at[p, j, at],
             send_sem=give_out.at[p, j], recv_sem=give_in.at[p, j],
             device_id=across, device_id_type=MESH,
         )
 
+    gives = [give(p, j) for p in range(2) for j in range(pairs)] if moved else []
+
     def line(o, j):
-        to = lax.rem(me + o, groups)
+        to = turned(o)
         return pltpu.make_async_remote_copy(
             src_ref=blocks.at[lax.div(to, 2), lax.rem(to, 2), j], dst_ref=lines.at[j, me],
             send_sem=line_out.at[j, o], recv_sem=line_in.at[j, o],
-            device_id={"grp": to, "slab": slab}, device_id_type=MESH,
+            device_id=place(to), device_id_type=MESH,
         )
 
     def stay(j):
         return pltpu.make_async_copy(blocks.at[chip, core, j], lines.at[j, me], own_sem.at[j])
 
     for j in range(pairs):
+        lig_loads[j].wait()
+
+        @pl.loop(0, chips)
+        def _(b):
+            for r in range(rotations):
+                for q in range(2):
+                    piece = lig[r, 2 * j + q, :, pl.ds(pl.multiple_of(b * block, block), block), :]
+                    blocks[b, r, j, q] = piece.reshape(lot, length).astype(bf16)
+
+        if j == 0:
+            pl.semaphore_wait(barrier, groups)
+
         @pl.loop(1, groups)
         def _(o):
             line(o, j).start()
 
         stay(j).start()
-    if moved:
-        for p in range(2):
-            for j in range(pairs):
-                give(p, j).start()
+    for copy in gives:
+        copy.start()
 
     def along_y(j, g):
         plane = dot(jnp.concatenate([lines[j, g, 0], lines[j, g, 1]], 1), fy_ref[...])
         for p in range(2):
-            at = pl.ds(pl.multiple_of(g * rows, rows), rows)
+            at = pl.ds(pl.multiple_of(g * lot, lot), lot)
             along[p, at, :] = plane[:, p * length : (p + 1) * length]
 
-    for j in range(pairs):
-        stay(j).wait()
-        along_y(j, me)
-
-        @pl.loop(1, groups)
-        def _(o):
-            line(o, j).wait_recv()
-            along_y(j, lax.rem(me + groups - o, groups))
-
+    def along_z():
         @pl.loop(0, block)
         def _(x):
             parts = [along[p, pl.ds(x, length, stride=block), :].astype(bf16) for p in range(2)]
             found = dot(fz_ref[slab], jnp.concatenate(parts, 0))
             for p in range(2):
                 at = pl.ds(pl.multiple_of((p * block + x) * length, length), length)
-                hold[at, :] = found[p * length : (p + 1) * length, :]
-
-        @pl.loop(0, half, unroll=4)
-        def _(k):
-            near_ref[k, j] = hold[pl.ds(k, 2 * block, stride=length), :].astype(bf16)
-            swap_ref[k, j] = hold[pl.ds(half + k, 2 * block, stride=length), :].astype(bf16)
-
-    for j in range(pairs):
-        @pl.loop(1, groups)
-        def _(o):
-            line(o, j).wait_send()
-
-    if moved:
-        for p in range(2):
-            for j in range(pairs):
-                give(p, j).wait()
-
-
-def score_kernel(
-    rotations, groups, length, chunks, moved, fx_ref, ix_ref, iy_ref, mz_ref, rec_ref, give_ref, near_ref, swap_ref, out_ref,
-    mine_ref, far_ref, held, rec, send, hold, rec_sem, near_sem, swap_out, swap_in, ring_out, ring_in, pair_out, pair_in, slab_out, slab_in,
-):
-    me = lax.axis_index("grp")
-    slab = lax.axis_index("slab")
-    core = lax.rem(me, 2)
-    half = length // 2
-    single = (half - 2 * moved) // SUB
-    lasting = single + moved // SUB
-    height = groups // 4
-    around = groups // 2
-    row = me // 4
-    column = lax.rem(me // 2, 2)
-    spot = jnp.where(column == 0, row, around - 1 - row)
-
-    def device(at, which):
-        at = lax.rem(at + around, around)
-        return jnp.where(at < height, at * 4, (around - 1 - at) * 4 + 2) + which
-
-    beside = (device(spot + 1, core), device(spot - 1, core))
-    partner = device(spot, 1 - core)
-
-    def place(to):
-        return {"grp": to, "slab": slab}
-
-    across = {"grp": me, "slab": 1 - slab}
-    MESH = pl.DeviceIdType.MESH
-    rest = half - 1 - moved
-    loads = [
-        pltpu.make_async_copy(from_ref, rec.at[:, :, pl.ds(at, many)], rec_sem.at[n])
-        for n, (from_ref, at, many) in enumerate(
-            [
-                (rec_ref.at[:, :, pl.ds(0, 1)], 0, 1),
-                (rec_ref.at[:, :, pl.ds(moved + 1, rest)], moved + 1, rest),
-            ]
-            + [(give_ref, 1, moved)] * (moved > 0)
-        )
-    ]
-    place_own = pltpu.make_async_copy(near_ref, held.at[me, slab], near_sem)
-    place_own.start()
-    for load in loads:
-        load.start()
-    barrier = pltpu.get_barrier_semaphore()
-    for to in (place(beside[0]), place(beside[1]), place(partner), across):
-        pl.semaphore_signal(barrier, inc=1, device_id=to, device_id_type=MESH)
-    pl.semaphore_wait(barrier, 4)
+                hold[0, at, :] = found[p * length : (p + 1) * length, :]
 
     def swap(c):
         at = pl.ds(c * SUB, SUB)
         return pltpu.make_async_remote_copy(
-            src_ref=swap_ref.at[at], dst_ref=held.at[me, slab, at],
+            src_ref=other.at[at], dst_ref=held.at[me, slab, at],
             send_sem=swap_out.at[c], recv_sem=swap_in.at[c],
             device_id=across, device_id_type=MESH,
         )
 
-    @pl.loop(0, chunks)
-    def _(c):
-        swap(c).start()
-
-    def join(c):
-        swap(c).wait_recv()
+    for j in range(pairs):
+        stay(j).wait()
+        along_y(j, me)
+
+        @pl.loop(1, groups)
+        def _(o):
+            line(o, j).wait_recv()
+            along_y(j, turned(-o))
+
+        along_z()
+
+        @pl.loop(0, chunks)
+        def _(c):
+            @pl.loop(0, SUB, unroll=4)
+            def _(n):
+                k = c * SUB + n
+                other[k, j] = hold[0, pl.ds(half + k, 2 * block, stride=length), :].astype(bf16)
+                held[me, slab, k, j] = hold[0, pl.ds(k, 2 * block, stride=length), :].astype(bf16)
+
+            if j == pairs - 1:
+                swap(c).start()
 
     def origin(d, t):
         return spot - t if d == 0 else spot + t
 
-    def part(slot, c):
-        return held.at[slot, :, pl.ds(c * SUB, SUB)]
+    def part(slot, c, d, t):
+        if t <= far_step:
+            return held.at[slot, :, pl.ds(c * SUB, SUB)]
+        return held.at[slot, :, pl.ds(c * SUB + d * (SUB // 2), SUB // 2)]
 
     def ring(d, c, t, slot):
         return pltpu.make_async_remote_copy(
-            src_ref=part(slot, c), dst_ref=part(slot, c),
+            src_ref=part(slot, c, d, t + 1), dst_ref=part(slot, c, d, t + 1),
             send_sem=ring_out.at[d, c, t], recv_sem=ring_in.at[d, c, t],
             device_id=place(beside[d]), device_id_type=MESH,
         )
@@ -321,7 +310,7 @@
     def pair(d, c, t, which):
         slot = device(origin(d, t), which)
         return pltpu.make_async_remote_copy(
-            src_ref=part(slot, c), dst_ref=part(slot, c),
+            src_ref=part(slot, c, d, t), dst_ref=part(slot, c, d, t),
             send_sem=pair_out.at[d, c, t], recv_sem=pair_in.at[d, c, t],
             device_id=place(partner), device_id_type=MESH,
         )
@@ -329,41 +318,36 @@
     def slab_copy(c, q):
         at = pl.ds(pl.multiple_of(q * TILE, TILE), TILE)
         return pltpu.make_async_remote_copy(
-            src_ref=send.at[c, :, at], dst_ref=far_ref.at[c, :, at],
+            src_ref=send.at[c, :, at], dst_ref=far.at[c, :, at],
             send_sem=slab_out.at[c, q], recv_sem=slab_in.at[c, q],
             device_id=across, device_id_type=MESH,
         )
 
-    far_step = around // 2 - 1
-
-    def for_far(c, act):
+    def open_chunk(c):
+        swap(c).wait_recv()
         for d in range(2):
-            @pl.when(lax.rem(c, 2) == d)
-            def _():
-                act(d)
+            ring_send(d, c, 0)
+        pair(0, c, 0, core).start()
 
     def arrived(c, t):
         for d in range(2):
             ring_wait(d, c, t)
-            if t + 1 < far_step:
+            if t < far_step:
                 ring_send(d, c, t + 1)
             pair(d, c, t + 1, core).start()
 
-    rows = rotations * length
-    chips = groups // 2
-
     def plane(z, slot):
-        kr = [rec[0, j, slot].astype(f32) for j in range(2)]
-        ki = [rec[1, j, slot].astype(f32) for j in range(2)]
+        kr = [rec[0, j, slot].astype(f32) for j in range(pairs)]
+        ki = [rec[1, j, slot].astype(f32) for j in range(pairs)]
         real, imag = [], []
         for r in range(rotations):
             cols = [
                 jnp.concatenate([held[2 * b + r, s, z, j] for b in range(chips) for s in range(2)], 0)
-                for j in range(2)
+                for j in range(pairs)
             ]
             spec = dot(fx_ref[...], jnp.concatenate(cols, 1))
-            sr = [spec[:length, j * length : (j + 1) * length] for j in range(2)]
-            si = [spec[length:, j * length : (j + 1) * length] for j in range(2)]
+            sr = [spec[:length, j * length : (j + 1) * length] for j in range(pairs)]
+            si = [spec[length:, j * length : (j + 1) * length] for j in range(pairs)]
             real.append(kr[0] * sr[0] - ki[0] * si[0] + (kr[1] * sr[1] - ki[1] * si[1]))
             imag.append(kr[0] * si[0] + ki[0] * sr[0] + (kr[1] * si[1] + ki[1] * sr[1]))
         product = jnp.concatenate(
@@ -413,13 +397,6 @@
                 at = pl.ds(r * length + first + x, SUB, stride=rows)
                 ref[c, r, x] = jnp.concatenate([hold[0, at, :], hold[1, at, :]], 0).astype(bf16)
 
-    def open_chunk(c):
-        for d in range(2):
-            ring_send(d, c, 0)
-        pair(0, c, 0, core).start()
-
-    place_own.wait()
-    join(0)
     open_chunk(0)
 
     @pl.loop(0, chunks + 2)
@@ -430,27 +407,20 @@
         def _():
             arrived(c1, 1)
 
-        @pl.when(i + 1 < chunks)
-        def _():
-            join(i + 1)
-
         @pl.when(i == 2)
         def _():
-            for load in loads:
+            for load in rec_loads:
                 load.wait()
+            for copy in gives:
+                copy.wait()
 
         @pl.when(c2 >= 0)
         def _():
-            def act(d):
-                ring_wait(d, c2, far_step)
-                pair(d, c2, far_step + 1, core).start()
-
-            for_far(c2, act)
+            arrived(c2, far_step)
             pair(0, c2, 0, 1 - core).wait_recv()
-            for t in range(1, far_step + 1):
+            for t in range(1, far_step + 2):
                 for d in range(2):
                     pair(d, c2, t, 1 - core).wait_recv()
-            for_far(c2, lambda d: pair(d, c2, far_step + 1, 1 - core).wait_recv())
             compute(c2, 0)
 
         @pl.when(i < chunks)
@@ -460,7 +430,6 @@
         @pl.when((c1 >= 0) & (c1 < chunks))
         def _():
             arrived(c1, 2)
-            for_far(c1, lambda d: ring_send(d, c1, far_step))
 
         @pl.when(i + 1 < chunks)
         def _():
@@ -475,23 +444,22 @@
             def _():
                 c = jnp.where(over < 0, c2, single + lax.div(jnp.maximum(over, 0), 2))
                 collect(c, send, half)
-                collect(c, mine_ref, 0)
+                collect(c, mine, 0)
                 for q in range(half // TILE):
                     slab_copy(c, q).start()
 
+    for j in range(pairs):
+        @pl.loop(1, groups)
+        def _(o):
+            line(o, j).wait_send()
+
     @pl.loop(0, chunks)
     def _(c):
-        for t in range(far_step):
+        for t in range(far_step + 1):
             for d in range(2):
                 ring(d, c, t, device(origin(d, t), core)).wait_send()
                 pair(d, c, t + 1, core).wait_send()
         pair(0, c, 0, core).wait_send()
-
-        def act(d):
-            ring(d, c, far_step, device(origin(d, far_step), core)).wait_send()
-            pair(d, c, far_step + 1, core).wait_send()
-
-        for_far(c, act)
         swap(c).wait_send()
 
     @pl.loop(0, half // TILE)
@@ -505,9 +473,7 @@
         def _(x):
             cols = []
             for r in range(rotations):
-                tiles = [
-                    ref[t, r, q * TILE + x] for ref in (mine_ref, far_ref) for t in range(lasting)
-                ]
+                tiles = [ref[t, r, q * TILE + x] for ref in (mine, far) for t in range(lasting)]
                 cols.append(jnp.concatenate(tiles, 0))
             scores = dot(mz_ref[slab], jnp.concatenate(cols, 1))
             best = scores[:, :length]
@@ -527,55 +493,39 @@
     half = length // 2
     chips = groups // 2
     block = width // chips
-    rows = depth * block
-    moved = MOVED
-    fz, fy, fx, ix, iy, mz = matrices(length, groups, moved)
+    lot = depth * block
+    chunks = half // SUB
+    hops = groups // 4
+    lasting = chunks - MOVED // SUB
+    part = (lasting, rotations, half, TILE, length)
+    rec = receptor_kernel[0]
     whole = pl.BlockSpec(memory_space=pltpu.VMEM)
     away = pl.BlockSpec(memory_space=pl.ANY)
     dma = pltpu.SemaphoreType.DMA
-    rec = receptor_kernel[0]
-
-    shape = jax.ShapeDtypeStruct((half, pairs, 2 * block, length), bf16)
-    given = jax.ShapeDtypeStruct((2, pairs, moved, length, length), bf16)
-    near, other, give = pl.pallas_call(
-        functools.partial(front_kernel, moved, groups),
-        out_shape=[shape, shape, given],
-        in_specs=[whole, away, whole, whole],
-        out_specs=[whole, whole, away],
+    best = pl.pallas_call(
+        functools.partial(dock_kernel, groups, MOVED),
+        out_shape=jax.ShapeDtypeStruct((length, half, length), bf16),
+        in_specs=[whole] * 6 + [away] * 2,
+        out_specs=whole,
         scratch_shapes=[
-            pltpu.VMEM((chips, rotations, pairs, 2, rows, length), bf16),
-            pltpu.VMEM((pairs, groups, 2, rows, length), bf16),
+            pltpu.VMEM(ligand_grids.shape, f32),
+            pltpu.VMEM((chips, rotations, pairs, 2, lot, length), bf16),
+            pltpu.VMEM((pairs, groups, 2, lot, length), bf16),
             pltpu.VMEM((2, block * length, length), f32),
-            pltpu.VMEM((2 * block * length, length), f32),
+            pltpu.VMEM((half, pairs, 2 * block, length), bf16),
+            pltpu.VMEM((groups, 2, half, pairs, 2 * block, length), bf16),
+            pltpu.VMEM(rec.shape, bf16),
+            pltpu.VMEM(part, bf16),
+            pltpu.VMEM(part, bf16),
+            pltpu.VMEM(part, bf16),
+            pltpu.VMEM((2, SUB * rotations * length, length), f32),
+            dma((pairs,)),
+            dma((2,)),
+            dma((pairs,)),
             dma((pairs, groups)),
             dma((pairs, groups)),
-            dma((pairs,)),
             dma((2, pairs)),
             dma((2, pairs)),
-        ],
-        compiler_params=pltpu.CompilerParams(
-            collective_id=1, has_side_effects=True, vmem_limit_bytes=24 * 2**20
-        ),
-    )(ligand_grids, rec, fy, fz)
-
-    chunks = half // SUB
-    hops = groups // 4
-    lasting = chunks - moved // SUB
-    part = (lasting, rotations, half, TILE, length)
-    best = pl.pallas_call(
-        functools.partial(score_kernel, rotations, groups, length, chunks, moved),
-        out_shape=jax.ShapeDtypeStruct((length, half, length), bf16),
-        in_specs=[whole] * 4 + [away] * 4,
-        out_specs=whole,
-        scratch_shapes=[
-            pltpu.VMEM(part, bf16),
-            pltpu.VMEM(part, bf16),
-            pltpu.VMEM((groups, 2, half, pairs, TILE, length), bf16),
-            pltpu.VMEM(rec.shape, bf16),
-            pltpu.VMEM(part, bf16),
-            pltpu.VMEM((2, SUB * rotations * length, length), f32),
-            dma((3,)),
-            dma,
             dma((chunks,)),
             dma((chunks,)),
             dma((2, chunks, hops)),
@@ -588,7 +538,7 @@
         compiler_params=pltpu.CompilerParams(
             collective_id=0, has_side_effects=True, vmem_limit_bytes=60 * 2**20
         ),
-    )(fx, ix, iy, mz, rec, give, near, other)
+    )(*matrices(length, groups, MOVED), ligand_grids, rec)
 
     return best[None]
 

time: 172 us -> 155 us (0.901)
  local copies, waits for them, and re-layouts: 12.5 us -> 3.08 us
  Pallas kernels: 159 us -> 152 us
    unnamed x15 -> x1, local copies, waits for them, and re-layouts: 12.5 us -> 3.08 us
    pallas_call x2 -> x1, Pallas kernels: 159 us -> 152 us  [quick_body(): pl.pallas_call(functools.partial(dock_kernel, groups, MOVED), out_shape=j...]
where the time goes in v2:
time: 155 us
  Pallas kernels  152 us (98%)
  local copies, waits for them, and re-layouts  3.08 us (2%)
    pallas_call x1, Pallas kernels, quick_body(): pl.pallas_call(functools.partial(dock_kernel, groups, MOVED), out_shape=j...  152 us

profile of v2, /device:TPU:0, one launch (start us, length us, event | category | flops | bytes accessed | tf_op | source)
XLA Modules:
  0.0 155.0 jit_solution(13200431405705170503)
XLA Ops:
  0.0 151.9 %shard_map.82 = bf16[128,64,128]{2,1,0:T(8,128)(2,1)} custom-call(bf16[2,256,256]{2,1,0:T(8,128)(2,1)} %constant.20.fz_ref, bf16[256,256]{1,0:T(8,128)(2,1)} %constant.21.fy_ref, bf16[256,256]{1,0:T(8,128)(2,1)} %constant.22.fx_ref, bf16[2,256,256]{2,1,0:T(8,128)(2,1)} %constant.23.ix_ref, bf16[256,256]{1,0:T(8,128)(2,1)} %constant.24.iy_ref, ...), custom_call_target="tpu_custom_call" | custom-call | tf_op jit(solution)/shard_map/pallas_call | solution.py:505
  152.0 3.1 %copy.10 = bf16[1,128,64,128]{3,2,1,0:T(8,128)(2,1)} copy(bf16[1,128,64,128]{3,2,1,0:T(8,128)(2,1)} %bitcast.3) | data formatting | bytes 4194304

commit v3 on v2

--- a/solution.py
+++ b/solution.py
@@ -136,7 +136,7 @@
 
 def dock_kernel(
     groups, moved, fz_ref, fy_ref, fx_ref, ix_ref, iy_ref, mz_ref, lig_ref, rec_ref, out_ref,
-    lig, blocks, lines, along, other, held, rec, mine, far, send, hold,
+    lig, blocks, lines, along, other, held, rec, mine, far, send, hold, tall,
     lig_sem, rec_sem, own_sem, line_out, line_in, give_out, give_in,
     swap_out, swap_in, ring_out, ring_in, pair_out, pair_in, slab_out, slab_in,
 ):
@@ -153,7 +153,7 @@
     chunks = half // SUB
     single = (half - 2 * moved) // SUB
     lasting = single + moved // SUB
-    rows = rotations * length
+    steps = rotations * chunks
     height = groups // 4
     around = groups // 2
     row = lax.div(me, 4)
@@ -177,8 +177,7 @@
     across = {"grp": me, "slab": 1 - slab}
 
     lig_loads = [
-        pltpu.make_async_copy(lig_ref.at[:, pl.ds(2 * j, 2)], lig.at[:, pl.ds(2 * j, 2)], lig_sem.at[j])
-        for j in range(pairs)
+        pltpu.make_async_copy(lig_ref.at[r], lig.at[r], lig_sem.at[r]) for r in range(rotations)
     ]
     rest = half - 1 - moved
     rec_loads = [
@@ -209,40 +208,41 @@
 
     gives = [give(p, j) for p in range(2) for j in range(pairs)] if moved else []
 
-    def line(o, j):
+    def line(o, r):
         to = turned(o)
         return pltpu.make_async_remote_copy(
-            src_ref=blocks.at[lax.div(to, 2), lax.rem(to, 2), j], dst_ref=lines.at[j, me],
-            send_sem=line_out.at[j, o], recv_sem=line_in.at[j, o],
+            src_ref=blocks.at[lax.div(to, 2), lax.rem(to, 2), r], dst_ref=lines.at[r, me],
+            send_sem=line_out.at[r, o], recv_sem=line_in.at[r, o],
             device_id=place(to), device_id_type=MESH,
         )
 
-    def stay(j):
-        return pltpu.make_async_copy(blocks.at[chip, core, j], lines.at[j, me], own_sem.at[j])
-
-    for j in range(pairs):
-        lig_loads[j].wait()
+    def stay(r):
+        return pltpu.make_async_copy(blocks.at[chip, core, r], lines.at[r, me], own_sem.at[r])
+
+    for r in range(rotations):
+        lig_loads[r].wait()
 
         @pl.loop(0, chips)
         def _(b):
-            for r in range(rotations):
+            for j in range(pairs):
                 for q in range(2):
                     piece = lig[r, 2 * j + q, :, pl.ds(pl.multiple_of(b * block, block), block), :]
-                    blocks[b, r, j, q] = piece.reshape(lot, length).astype(bf16)
-
-        if j == 0:
+                    blocks[b, j, r, q] = piece.reshape(lot, length).astype(bf16)
+
+        if r == 0:
             pl.semaphore_wait(barrier, groups)
 
         @pl.loop(1, groups)
         def _(o):
-            line(o, j).start()
-
-        stay(j).start()
-    for copy in gives:
-        copy.start()
-
-    def along_y(j, g):
-        plane = dot(jnp.concatenate([lines[j, g, 0], lines[j, g, 1]], 1), fy_ref[...])
+            line(o, r).start()
+
+        stay(r).start()
+        if r == 0:
+            for copy in gives[:pairs]:
+                copy.start()
+
+    def along_y(r, g):
+        plane = dot(jnp.concatenate([lines[r, g, 0], lines[r, g, 1]], 1), fy_ref[...])
         for p in range(2):
             at = pl.ds(pl.multiple_of(g * lot, lot), lot)
             along[p, at, :] = plane[:, p * length : (p + 1) * length]
@@ -254,7 +254,7 @@
             found = dot(fz_ref[slab], jnp.concatenate(parts, 0))
             for p in range(2):
                 at = pl.ds(pl.multiple_of((p * block + x) * length, length), length)
-                hold[0, at, :] = found[p * length : (p + 1) * length, :]
+                tall[at, :] = found[p * length : (p + 1) * length, :]
 
     def swap(c):
         at = pl.ds(c * SUB, SUB)
@@ -264,14 +264,14 @@
             device_id=across, device_id_type=MESH,
         )
 
-    for j in range(pairs):
-        stay(j).wait()
-        along_y(j, me)
+    def front(r):
+        stay(r).wait()
+        along_y(r, me)
 
         @pl.loop(1, groups)
         def _(o):
-            line(o, j).wait_recv()
-            along_y(j, turned(-o))
+            line(o, r).wait_recv()
+            along_y(r, turned(-o))
 
         along_z()
 
@@ -280,11 +280,10 @@
             @pl.loop(0, SUB, unroll=4)
             def _(n):
                 k = c * SUB + n
-                other[k, j] = hold[0, pl.ds(half + k, 2 * block, stride=length), :].astype(bf16)
-                held[me, slab, k, j] = hold[0, pl.ds(k, 2 * block, stride=length), :].astype(bf16)
-
-            if j == pairs - 1:
-                swap(c).start()
+                other[r * half + k] = tall[pl.ds(half + k, 2 * block, stride=length), :].astype(bf16)
+                held[me, slab, r * half + k] = tall[pl.ds(k, 2 * block, stride=length), :].astype(bf16)
+
+            swap(r * chunks + c).start()
 
     def origin(d, t):
         return spot - t if d == 0 else spot + t
@@ -318,7 +317,7 @@
     def slab_copy(c, q):
         at = pl.ds(pl.multiple_of(q * TILE, TILE), TILE)
         return pltpu.make_async_remote_copy(
-            src_ref=send.at[c, :, at], dst_ref=far.at[c, :, at],
+            src_ref=send.at[c, at], dst_ref=far.at[c, at],
             send_sem=slab_out.at[c, q], recv_sem=slab_in.at[c, q],
             device_id=across, device_id_type=MESH,
         )
@@ -336,155 +335,167 @@
                 ring_send(d, c, t + 1)
             pair(d, c, t + 1, core).start()
 
-    def plane(z, slot):
+    def product(z, slot):
         kr = [rec[0, j, slot].astype(f32) for j in range(pairs)]
         ki = [rec[1, j, slot].astype(f32) for j in range(pairs)]
-        real, imag = [], []
-        for r in range(rotations):
-            cols = [
-                jnp.concatenate([held[2 * b + r, s, z, j] for b in range(chips) for s in range(2)], 0)
-                for j in range(pairs)
-            ]
-            spec = dot(fx_ref[...], jnp.concatenate(cols, 1))
-            sr = [spec[:length, j * length : (j + 1) * length] for j in range(pairs)]
-            si = [spec[length:, j * length : (j + 1) * length] for j in range(pairs)]
-            real.append(kr[0] * sr[0] - ki[0] * si[0] + (kr[1] * sr[1] - ki[1] * si[1]))
-            imag.append(kr[0] * si[0] + ki[0] * sr[0] + (kr[1] * si[1] + ki[1] * sr[1]))
-        product = jnp.concatenate(
-            [jnp.concatenate(real, 1).astype(bf16), jnp.concatenate(imag, 1).astype(bf16)], 0
-        )
-        done = dot(ix_ref[slab], product).astype(bf16)
+        cols = [
+            jnp.concatenate([held[2 * b + j, s, z] for b in range(chips) for s in range(2)], 0)
+            for j in range(pairs)
+        ]
+        spec = dot(fx_ref[...], jnp.concatenate(cols, 1))
+        sr = [spec[:length, j * length : (j + 1) * length] for j in range(pairs)]
+        si = [spec[length:, j * length : (j + 1) * length] for j in range(pairs)]
+        real = kr[0] * sr[0] - ki[0] * si[0] + (kr[1] * sr[1] - ki[1] * si[1])
+        imag = kr[0] * si[0] + ki[0] * sr[0] + (kr[1] * si[1] + ki[1] * sr[1])
+        return real.astype(bf16), imag.astype(bf16)
+
+    def planes(both):
+        parts = [product(z, slot) for z, slot in both]
+        joined = jnp.concatenate([jnp.concatenate([part[p] for part in parts], 1) for p in range(2)], 0)
+        done = dot(ix_ref[slab], joined).astype(bf16)
         flat = []
-        for r in range(rotations):
-            at = slice(r * length, (r + 1) * length)
+        for n in range(len(both)):
+            at = slice(n * length, (n + 1) * length)
             flat.append(jnp.concatenate([done[:length, at], done[length:, at]], 1))
         return dot(jnp.concatenate(flat, 0), iy_ref[...])
 
-    def keep(k, parts):
-        for p in range(2):
-            hold[p, pl.ds(pl.multiple_of(k * rows, rows), rows), :] = parts[p]
-
-    def alone(c, first):
-        @pl.loop(first, first + SUB // 2, unroll=2)
-        def _(k):
-            z = c * SUB + k
-            both = plane(z, jnp.where(z == 0, 0, z + moved))
-            keep(k, [both[:, :length], both[:, length:]])
-
-    def mirrored(c, first):
-        @pl.loop(0, SUB // 4)
-        def _(q):
-            z = c * SUB + first + 2 * q
-            n = lax.div(z - single * SUB, 2)
-            one = plane(z, half - moved + n)
-            two = plane(z + 1, moved - n)
-            keep(lax.rem(n, SUB), [one[:, :length] + two[:, :length], one[:, length:] - two[:, length:]])
-
-    def compute(c, first):
+    def compute(s):
+        c = lax.rem(s, chunks)
+
         @pl.when(c < single)
         def _():
-            alone(c, first)
+            @pl.loop(0, SUB // 2, unroll=2)
+            def _(n):
+                both = []
+                for k in (2 * n, 2 * n + 1):
+                    z = c * SUB + k
+                    both.append((s * SUB + k, jnp.where(z == 0, 0, z + moved)))
+                found = planes(both)
+                for p in range(2):
+                    at = pl.ds(pl.multiple_of(2 * n * length, 2 * length), 2 * length)
+                    hold[p, at, :] = found[:, p * length : (p + 1) * length]
 
         if moved:
             @pl.when(c >= single)
             def _():
-                mirrored(c, first)
-
-    def collect(c, ref, first):
+                @pl.loop(0, SUB // 2)
+                def _(n):
+                    z = s * SUB + 2 * n
+                    m = (c - single) * (SUB // 2) + n
+                    found = planes([(z, half - moved + m), (z + 1, moved - m)])
+                    one, two = found[:length], found[length:]
+                    at = pl.ds(pl.multiple_of(lax.rem(m, SUB) * length, length), length)
+                    hold[0, at, :] = one[:, :length] + two[:, :length]
+                    hold[1, at, :] = one[:, length:] - two[:, length:]
+
+    def collect(t, ref, first):
         @pl.loop(0, half, unroll=4)
         def _(x):
-            for r in range(rotations):
-                at = pl.ds(r * length + first + x, SUB, stride=rows)
-                ref[c, r, x] = jnp.concatenate([hold[0, at, :], hold[1, at, :]], 0).astype(bf16)
-
-    open_chunk(0)
-
-    @pl.loop(0, chunks + 2)
-    def _(i):
-        c1, c2 = i - 1, i - 2
-
-        @pl.when((c1 >= 0) & (c1 < chunks))
-        def _():
-            arrived(c1, 1)
-
-        @pl.when(i == 2)
-        def _():
-            for load in rec_loads:
-                load.wait()
-            for copy in gives:
-                copy.wait()
-
-        @pl.when(c2 >= 0)
-        def _():
-            arrived(c2, far_step)
-            pair(0, c2, 0, 1 - core).wait_recv()
-            for t in range(1, far_step + 2):
-                for d in range(2):
-                    pair(d, c2, t, 1 - core).wait_recv()
-            compute(c2, 0)
-
-        @pl.when(i < chunks)
-        def _():
-            arrived(i, 0)
-
-        @pl.when((c1 >= 0) & (c1 < chunks))
-        def _():
-            arrived(c1, 2)
-
-        @pl.when(i + 1 < chunks)
-        def _():
-            open_chunk(i + 1)
-
-        @pl.when(c2 >= 0)
-        def _():
-            compute(c2, SUB // 2)
-            over = c2 - single
-
-            @pl.when((over < 0) | (lax.rem(jnp.maximum(over, 0), 2) == 1))
-            def _():
-                c = jnp.where(over < 0, c2, single + lax.div(jnp.maximum(over, 0), 2))
-                collect(c, send, half)
-                collect(c, mine, 0)
-                for q in range(half // TILE):
-                    slab_copy(c, q).start()
-
-    for j in range(pairs):
-        @pl.loop(1, groups)
-        def _(o):
-            line(o, j).wait_send()
-
-    @pl.loop(0, chunks)
-    def _(c):
-        for t in range(far_step + 1):
-            for d in range(2):
-                ring(d, c, t, device(origin(d, t), core)).wait_send()
-                pair(d, c, t + 1, core).wait_send()
-        pair(0, c, 0, core).wait_send()
-        swap(c).wait_send()
-
-    @pl.loop(0, half // TILE)
-    def _(q):
-        @pl.loop(0, lasting)
-        def _(c):
-            slab_copy(c, q).wait_send()
-            slab_copy(c, q).wait_recv()
-
-        @pl.loop(0, TILE, unroll=2)
-        def _(x):
+            at = pl.ds(first + x, SUB, stride=length)
+            ref[t, x] = jnp.concatenate([hold[0, at, :], hold[1, at, :]], 0).astype(bf16)
+
+    def hand_over(s):
+        r, c = lax.div(s, chunks), lax.rem(s, chunks)
+        over = c - single
+
+        @pl.when((over < 0) | (lax.rem(jnp.maximum(over, 0), 2) == 1))
+        def _():
+            t = r * lasting + jnp.where(over < 0, c, single + lax.div(jnp.maximum(over, 0), 2))
+            collect(t, send, half)
+            for q in range(half // TILE):
+                slab_copy(t, q).start()
+            collect(t, mine, 0)
+
+    def score(r, q):
+        @pl.loop(r * lasting, (r + 1) * lasting)
+        def _(t):
+            slab_copy(t, q).wait_send()
+            slab_copy(t, q).wait_recv()
+
+        @pl.loop(0, TILE // 2, unroll=2)
+        def _(n):
             cols = []
-            for r in range(rotations):
-                tiles = [ref[t, r, q * TILE + x] for ref in (mine, far) for t in range(lasting)]
+            for x in (2 * n, 2 * n + 1):
+                tiles = [ref[r * lasting + t, q * TILE + x] for ref in (mine, far) for t in range(lasting)]
                 cols.append(jnp.concatenate(tiles, 0))
-            scores = dot(mz_ref[slab], jnp.concatenate(cols, 1))
-            best = scores[:, :length]
-            for r in range(1, rotations):
-                best = jnp.maximum(best, scores[:, r * length : (r + 1) * length])
-            hold[0, pl.ds(x * length, length), :] = best
+            found = dot(mz_ref[slab], jnp.concatenate(cols, 1))
+            for x in range(2):
+                at = pl.ds(pl.multiple_of((2 * n + x) * length, length), length)
+                tall[at, :] = found[:, x * length : (x + 1) * length]
 
         @pl.loop(0, length, unroll=4)
         def _(z):
             at = pl.ds(pl.multiple_of(q * TILE, TILE), TILE)
-            out_ref[z, at, :] = hold[0, pl.ds(z, TILE, stride=length), :].astype(bf16)
+            best = tall[pl.ds(z, TILE, stride=length), :]
+            if r > 0:
+                best = jnp.maximum(out_ref[z, at, :].astype(f32), best)
+            out_ref[z, at, :] = best.astype(bf16)
+
+    front(0)
+    for copy in gives[pairs:]:
+        copy.start()
+    open_chunk(0)
+    early = half // TILE
+    begin = steps + far_step - early - 2
+
+    @pl.loop(0, steps + far_step)
+    def _(i):
+        @pl.when(i + 1 < steps)
+        def _():
+            open_chunk(i + 1)
+
+        for t in range(far_step - 1, -1, -1):
+            @pl.when((i >= t) & (i - t < steps))
+            def _():
+                arrived(i - t, t)
+
+        @pl.when(i == far_step)
+        def _():
+            for load in rec_loads:
+                load.wait()
+
+        if moved:
+            @pl.when(i == far_step + single)
+            def _():
+                for copy in gives:
+                    copy.wait()
+
+        @pl.when(i >= far_step)
+        def _():
+            s = i - far_step
+            arrived(s, far_step)
+            pair(0, s, 0, 1 - core).wait_recv()
+            for t in range(1, far_step + 2):
+                for d in range(2):
+                    pair(d, s, t, 1 - core).wait_recv()
+            compute(s)
+            hand_over(s)
+
+        @pl.when(i == far_step)
+        def _():
+            front(1)
+
+        @pl.when((i >= begin) & (i < begin + early))
+        def _():
+            score(0, i - begin)
+
+    for r in range(rotations):
+        @pl.loop(1, groups)
+        def _(o):
+            line(o, r).wait_send()
+
+    @pl.loop(0, steps)
+    def _(s):
+        for t in range(far_step + 1):
+            for d in range(2):
+                ring(d, s, t, device(origin(d, t), core)).wait_send()
+                pair(d, s, t + 1, core).wait_send()
+        pair(0, s, 0, core).wait_send()
+        swap(s).wait_send()
+
+    @pl.loop(0, half // TILE)
+    def _(q):
+        score(1, q)
 
 
 def quick_body(groups, ligand_grids, receptor_kernel):
@@ -497,7 +508,8 @@
     chunks = half // SUB
     hops = groups // 4
     lasting = chunks - MOVED // SUB
-    part = (lasting, rotations, half, TILE, length)
+    steps = rotations * chunks
+    part = (rotations * lasting, half, TILE, length)
     rec = receptor_kernel[0]
     whole = pl.BlockSpec(memory_space=pltpu.VMEM)
     away = pl.BlockSpec(memory_space=pl.ANY)
@@ -509,31 +521,32 @@
         out_specs=whole,
         scratch_shapes=[
             pltpu.VMEM(ligand_grids.shape, f32),
-            pltpu.VMEM((chips, rotations, pairs, 2, lot, length), bf16),
-            pltpu.VMEM((pairs, groups, 2, lot, length), bf16),
+            pltpu.VMEM((chips, pairs, rotations, 2, lot, length), bf16),
+            pltpu.VMEM((rotations, groups, 2, lot, length), bf16),
             pltpu.VMEM((2, block * length, length), f32),
-            pltpu.VMEM((half, pairs, 2 * block, length), bf16),
-            pltpu.VMEM((groups, 2, half, pairs, 2 * block, length), bf16),
+            pltpu.VMEM((rotations * half, 2 * block, length), bf16),
+            pltpu.VMEM((groups, 2, rotations * half, 2 * block, length), bf16),
             pltpu.VMEM(rec.shape, bf16),
             pltpu.VMEM(part, bf16),
             pltpu.VMEM(part, bf16),
             pltpu.VMEM(part, bf16),
-            pltpu.VMEM((2, SUB * rotations * length, length), f32),
-            dma((pairs,)),
+            pltpu.VMEM((2, SUB * length, length), f32),
+            pltpu.VMEM((TILE * length, length), f32),
+            dma((rotations,)),
             dma((2,)),
-            dma((pairs,)),
-            dma((pairs, groups)),
-            dma((pairs, groups)),
+            dma((rotations,)),
+            dma((rotations, groups)),
+            dma((rotations, groups)),
             dma((2, pairs)),
             dma((2, pairs)),
-            dma((chunks,)),
-            dma((chunks,)),
-            dma((2, chunks, hops)),
-            dma((2, chunks, hops)),
-            dma((2, chunks, hops + 1)),
-            dma((2, chunks, hops + 1)),
-            dma((lasting, half // TILE)),
-            dma((lasting, half // TILE)),
+            dma((steps,)),
+            dma((steps,)),
+            dma((2, steps, hops)),
+            dma((2, steps, hops)),
+            dma((2, steps, hops + 1)),
+            dma((2, steps, hops + 1)),
+            dma((rotations * lasting, half // TILE)),
+            dma((rotations * lasting, half // TILE)),
         ],
         compiler_params=pltpu.CompilerParams(
             collective_id=0, has_side_effects=True, vmem_limit_bytes=60 * 2**20

time: 155 us -> 162 us (1.045)
  Pallas kernels: 152 us -> 158 us
    pallas_call x1, Pallas kernels: 152 us -> 158 us  [quick_body(): pl.pallas_call(functools.partial(dock_kernel, groups, MOVED), out_shape=j...]
where the time goes in v3:
time: 162 us; the launch traced here: 161 us
  Pallas kernels  158 us (98%)
  local copies, waits for them, and re-layouts  3.08 us (2%)
    pallas_call x1, Pallas kernels, quick_body(): pl.pallas_call(functools.partial(dock_kernel, groups, MOVED), out_shape=j...  158 us

profile of v3, /device:TPU:0, one launch (start us, length us, event | category | flops | bytes accessed | tf_op | source)
XLA Modules:
  0.0 161.5 jit_solution(2099784160658358037)
XLA Ops:
  0.0 158.4 %shard_map.82 = bf16[128,64,128]{2,1,0:T(8,128)(2,1)} custom-call(bf16[2,256,256]{2,1,0:T(8,128)(2,1)} %constant.20.fz_ref, bf16[256,256]{1,0:T(8,128)(2,1)} %constant.21.fy_ref, bf16[256,256]{1,0:T(8,128)(2,1)} %constant.22.fx_ref, bf16[2,256,256]{2,1,0:T(8,128)(2,1)} %constant.23.ix_ref, bf16[256,256]{1,0:T(8,128)(2,1)} %constant.24.iy_ref, ...), custom_call_target="tpu_custom_call" | custom-call | tf_op jit(solution)/shard_map/pallas_call | solution.py:517
  158.4 3.1 %copy.10 = bf16[1,128,64,128]{3,2,1,0:T(8,128)(2,1)} copy(bf16[1,128,64,128]{3,2,1,0:T(8,128)(2,1)} %bitcast.3) | data formatting | bytes 4194304

commit v4 on v2

--- a/solution.py
+++ b/solution.py
@@ -81,7 +81,8 @@
 
 TILE = 16
 SUB = 8
-MOVED = 8
+MOVED = 16
+AHEAD = 1
 f32 = jnp.float32
 bf16 = jnp.bfloat16
 
@@ -238,7 +239,7 @@
             line(o, j).start()
 
         stay(j).start()
-    for copy in gives:
+    for copy in gives[:pairs]:
         copy.start()
 
     def along_y(j, g):
@@ -320,6 +321,13 @@
         return pltpu.make_async_remote_copy(
             src_ref=send.at[c, :, at], dst_ref=far.at[c, :, at],
             send_sem=slab_out.at[c, q], recv_sem=slab_in.at[c, q],
+            device_id=across, device_id_type=MESH,
+        )
+
+    def slab_whole(c):
+        return pltpu.make_async_remote_copy(
+            src_ref=send.at[c], dst_ref=far.at[c],
+            send_sem=slab_out.at[c, 0], recv_sem=slab_in.at[c, 0],
             device_id=across, device_id_type=MESH,
         )
 
@@ -397,7 +405,10 @@
                 at = pl.ds(r * length + first + x, SUB, stride=rows)
                 ref[c, r, x] = jnp.concatenate([hold[0, at, :], hold[1, at, :]], 0).astype(bf16)
 
-    open_chunk(0)
+    for copy in gives[pairs:]:
+        copy.start()
+    for c in range(AHEAD):
+        open_chunk(c)
 
     @pl.loop(0, chunks + 2)
     def _(i):
@@ -411,8 +422,12 @@
         def _():
             for load in rec_loads:
                 load.wait()
-            for copy in gives:
-                copy.wait()
+
+        if moved:
+            @pl.when(i == 2 + single)
+            def _():
+                for copy in gives:
+                    copy.wait()
 
         @pl.when(c2 >= 0)
         def _():
@@ -431,9 +446,9 @@
         def _():
             arrived(c1, 2)
 
-        @pl.when(i + 1 < chunks)
-        def _():
-            open_chunk(i + 1)
+        @pl.when(i + AHEAD < chunks)
+        def _():
+            open_chunk(i + AHEAD)
 
         @pl.when(c2 >= 0)
         def _():
@@ -444,9 +459,17 @@
             def _():
                 c = jnp.where(over < 0, c2, single + lax.div(jnp.maximum(over, 0), 2))
                 collect(c, send, half)
+
+                @pl.when(c < lasting - 1)
+                def _():
+                    slab_whole(c).start()
+
+                @pl.when(c == lasting - 1)
+                def _():
+                    for q in range(half // TILE):
+                        slab_copy(lasting - 1, q).start()
+
                 collect(c, mine, 0)
-                for q in range(half // TILE):
-                    slab_copy(c, q).start()
 
     for j in range(pairs):
         @pl.loop(1, groups)
@@ -464,10 +487,15 @@
 
     @pl.loop(0, half // TILE)
     def _(q):
-        @pl.loop(0, lasting)
-        def _(c):
-            slab_copy(c, q).wait_send()
-            slab_copy(c, q).wait_recv()
+        @pl.when(q == 0)
+        def _():
+            @pl.loop(0, lasting - 1)
+            def _(c):
+                slab_whole(c).wait_send()
+                slab_whole(c).wait_recv()
+
+        slab_copy(lasting - 1, q).wait_send()
+        slab_copy(lasting - 1, q).wait_recv()
 
         @pl.loop(0, TILE, unroll=2)
         def _(x):

time: 155 us -> 153 us (0.987)
  Pallas kernels: 152 us -> 149 us
    pallas_call x1, Pallas kernels: 152 us -> 149 us  [quick_body(): pl.pallas_call(functools.partial(dock_kernel, groups, MOVED), out_shape=j...]
where the time goes in v4:
time: 153 us; the launch traced here: 152 us
  Pallas kernels  149 us (97%)
  local copies, waits for them, and re-layouts  3.08 us (2%)
    pallas_call x1, Pallas kernels, quick_body(): pl.pallas_call(functools.partial(dock_kernel, groups, MOVED), out_shape=j...  149 us
    unnamed x1, local copies, waits for them, and re-layouts  3.08 us

profile of v4, /device:TPU:0, one launch (start us, length us, event | category | flops | bytes accessed | tf_op | source)
XLA Modules:
  0.0 152.0 jit_solution(7309488403132423440)
XLA Ops:
  0.0 148.9 %shard_map.82 = bf16[128,64,128]{2,1,0:T(8,128)(2,1)} custom-call(bf16[2,256,256]{2,1,0:T(8,128)(2,1)} %constant.20.fz_ref, bf16[256,256]{1,0:T(8,128)(2,1)} %constant.21.fy_ref, bf16[256,256]{1,0:T(8,128)(2,1)} %constant.22.fx_ref, bf16[2,256,256]{2,1,0:T(8,128)(2,1)} %constant.23.ix_ref, bf16[256,256]{1,0:T(8,128)(2,1)} %constant.24.iy_ref, ...), custom_call_target="tpu_custom_call" | custom-call | tf_op jit(solution)/shard_map/pallas_call | solution.py:533
  148.9 3.1 %copy.10 = bf16[1,128,64,128]{3,2,1,0:T(8,128)(2,1)} copy(bf16[1,128,64,128]{3,2,1,0:T(8,128)(2,1)} %bitcast.3) | data formatting | bytes 4194304
